TPU v7x, 128 devices: a whole 4x4x4 slice. The times are simulated.
128 devices in a mesh: ctx: 16 (over y, z), pack: 8 (over x, core).
Axes of the slice: x: 4, y: 4, z: 4, core: 2. Of those that a mesh axis runs over, the one named last changes fastest.
Arguments:
- hidden: bfloat16 [32768, 2048], P(('ctx', 'pack')), may hold values from -4 to 4
- first_keys: bfloat16 [32768, 2048], P('ctx', 'pack'), may hold values from -400 to 400
- first_values: bfloat16 [32768, 2048], P('ctx', 'pack'), may hold values from -18 to 18
- w_query: bfloat16 [2048, 2048], P(None, 'pack'), may hold values from -0.125 to 0.125
- w_out: bfloat16 [2048, 2048], P('pack'), may hold values from -0.125 to 0.125
- norm_gain: float32 [2048], replicated, may hold values from 0.1 to 1.9
- router_weight: float32 [2048], replicated, may hold values from -0.5 to 0.5
- route_list: int32 [16, 512], P('ctx'), may hold values from 0 to 2047, as said below
- pack_order: int32 [16, 512], P('ctx'), may hold values from 0 to 511, each once within a row
- pattern: int32 [16, 12], replicated, may hold values from 0 to 15
Outputs:
- hidden_out: bfloat16 [32768, 2048], P(('ctx', 'pack'))
- packed_states: bfloat16 [8192, 2048], P(('ctx', 'pack'))
Inputs may be any that keep to these rules, and one draw needn't show every extreme that they name: `route_list`: each row lists 512 distinct span-local positions in ascending order. At most 96 of a row's positions lie among the 256 tokens of one device, and in every row some device holds exactly 96.
All inputs are finite; a program needn't handle non-finite values.
Results may differ from a plain program's by a relative error of at most 0.023.
Values may be sent and summed in bfloat16 or wider, within the bound.
A program may use at most 128 MiB of HBM per device.

v0:
```python
import math

import jax
import jax.numpy as jnp
from jax import lax
from jax.sharding import PartitionSpec as P

HD = 128


epsilon = 1e-06
very_negative = -1e30


def rotate(projected, position, head_count):
    row_count = projected.shape[0]
    head_size = projected.shape[1] // head_count
    half_size = head_size // 2
    frequency = 10000.0 ** (-jnp.arange(half_size, dtype=jnp.float32) * 2.0 / head_size)
    angle = position.astype(jnp.float32)[:, None] * frequency[None, :]
    cosine = jnp.cos(angle)[:, None, :]
    sine_part = jnp.sin(angle)[:, None, :]
    shaped = projected.reshape(row_count, head_count, head_size)
    front_half = shaped[..., :half_size]
    back_half = shaped[..., half_size:]
    turned = jnp.concatenate(
        [front_half * cosine - back_half * sine_part, back_half * cosine + front_half * sine_part],
        axis=-1,
    )
    return turned.reshape(row_count, head_count * head_size)


def partial_block(query_heads, key_heads, value_heads, allowed):
    scale_factor = 1.0 / math.sqrt(query_heads.shape[2])
    scores = (
        jnp.einsum("qhd,khd->hqk", query_heads, key_heads, preferred_element_type=jnp.float32)
        * scale_factor
    )
    if allowed is not None:
        scores = jnp.where(allowed[None], scores, very_negative)
    row_peak = jnp.max(scores, axis=-1)
    weights = jnp.exp(scores - row_peak[..., None])
    if allowed is not None:
        weights = jnp.where(allowed[None], weights, 0.0)
    weight_sum = jnp.sum(weights, axis=-1)
    rounded = weights.astype(jnp.bfloat16)
    summed = jnp.einsum("hqk,khd->qhd", rounded, value_heads, preferred_element_type=jnp.float32)
    return (row_peak, weight_sum, summed)


def merge(former, latter):
    new_peak = jnp.maximum(former[0], latter[0])
    former_scale = jnp.exp(former[0] - new_peak)
    latter_scale = jnp.exp(latter[0] - new_peak)
    weight_sum = former_scale * former[1] + latter_scale * latter[1]
    summed = (
        jnp.transpose(former_scale)[:, :, None] * former[2]
        + jnp.transpose(latter_scale)[:, :, None] * latter[2]
    )
    return (new_peak, weight_sum, summed)


def local(
    hidden,
    first_keys,
    first_values,
    w_query,
    w_out,
    norm_gain,
    router_weight,
    route_list,
    pack_order,
    pattern,
):
    n_pack = lax.axis_size("pack")
    span_id = lax.axis_index("ctx")
    pack_id = lax.axis_index("pack")
    tok_dev = hidden.shape[0]
    model_width = hidden.shape[1]
    span_len = tok_dev * n_pack
    routes = route_list[0]
    slot_order = pack_order[0]
    routed = routes.shape[0]
    per_slot = routed // n_pack
    capacity = 3 * tok_dev // 8
    local_width = first_keys.shape[1]
    head_count = local_width // HD
    lane_ids = jnp.arange(n_pack, dtype=jnp.int32)
    starts = jnp.sum((routes[None, :] < (lane_ids * tok_dev)[:, None]).astype(jnp.int32), axis=1)
    run_ends = jnp.concatenate([starts[1:], jnp.full((1,), routed, jnp.int32)])
    my_start = jnp.sum(jnp.where(lane_ids == pack_id, starts, 0))
    my_count = jnp.sum(jnp.where(lane_ids == pack_id, run_ends - starts, 0))
    padded = jnp.concatenate([routes, jnp.full((capacity,), span_len, jnp.int32)])
    sending = lax.dynamic_slice_in_dim(padded, my_start, capacity, 0)
    is_valid = jnp.arange(capacity, dtype=jnp.int32) < my_count
    local_rows = jnp.clip(sending - pack_id * tok_dev, 0, tok_dev - 1)
    outgoing = jnp.where(is_valid[:, None], hidden[local_rows], jnp.zeros((), hidden.dtype))
    gathered = lax.all_gather(outgoing, "pack", axis=0, tiled=True)
    picked = routes[slot_order]
    owner_id = picked // tok_dev
    owner_start = jnp.sum(
        jnp.where(owner_id[:, None] == lane_ids[None, :], starts[None, :], 0), axis=1
    )
    source_row = owner_id * capacity + (slot_order - owner_start)
    routed_rows = gathered[source_row]
    position = span_id * span_len + picked
    rows_float = routed_rows.astype(jnp.float32)
    mean_square = jnp.mean(rows_float * rows_float, axis=-1, keepdims=True)
    normed = (rows_float * lax.rsqrt(mean_square + epsilon) * norm_gain).astype(jnp.bfloat16)
    queries = rotate(
        jnp.dot(normed, w_query, preferred_element_type=jnp.float32), position, head_count
    ).astype(jnp.bfloat16)
    query_heads = queries.reshape(routed, head_count, HD)
    key_heads = first_keys.reshape(span_len, head_count, HD)
    value_heads = first_values.reshape(span_len, head_count, HD)
    key_pos = span_id * span_len + jnp.arange(span_len, dtype=jnp.int32)
    own_state = partial_block(
        query_heads, key_heads, value_heads, key_pos[None, :] <= position[:, None]
    )
    wanted = pattern[span_id]
    running = own_state
    key_piece = lax.all_gather(first_keys, "ctx", axis=0, tiled=True)
    value_piece = lax.all_gather(first_values, "ctx", axis=0, tiled=True)
    blocks = key_piece.shape[0] // span_len
    key_stack = key_piece.reshape(blocks, span_len, head_count, HD)
    value_stack = value_piece.reshape(blocks, span_len, head_count, HD)

    def visit(held, block_item):
        block_idx, key_block, value_block = block_item
        active = jnp.logical_and(block_idx < span_id, jnp.any(wanted == block_idx))
        held = lax.cond(
            active,
            lambda inner: merge(inner, partial_block(query_heads, key_block, value_block, None)),
            lambda inner: inner,
            held,
        )
        return (held, None)

    running, unused = lax.scan(
        visit, running, (jnp.arange(blocks, dtype=jnp.int32), key_stack, value_stack)
    )
    attended = (
        (running[2] / jnp.transpose(running[1])[:, :, None])
        .reshape(routed, local_width)
        .astype(jnp.bfloat16)
    )
    mixed = lax.psum_scatter(
        jnp.dot(attended, w_out, preferred_element_type=jnp.float32),
        "pack",
        scatter_dimension=0,
        tiled=True,
    )
    own_rows = lax.dynamic_slice_in_dim(rows_float, pack_id * per_slot, per_slot, 0)
    gate_value = jax.nn.sigmoid(jnp.dot(own_rows, router_weight, precision=lax.Precision.HIGHEST))
    packed_states = (own_rows + gate_value[:, None] * mixed).astype(jnp.bfloat16)
    target = jnp.where(is_valid, sending - pack_id * tok_dev, tok_dev)
    slot_rows = lax.dynamic_slice_in_dim(source_row, pack_id * per_slot, per_slot, 0)
    returning = (
        jnp.zeros((n_pack * capacity, model_width), jnp.float32)
        .at[slot_rows]
        .set(packed_states.astype(jnp.float32))
    )
    arrived = lax.psum_scatter(
        returning.astype(jnp.bfloat16), "pack", scatter_dimension=0, tiled=True
    )
    hidden_out = hidden.at[target].set(arrived, mode="drop")
    return (hidden_out, packed_states)


def solution(mesh):
    return jax.shard_map(
        local,
        mesh=mesh,
        in_specs=(
            P(("ctx", "pack"), None),
            P("ctx", "pack"),
            P("ctx", "pack"),
            P(None, "pack"),
            P("pack", None),
            P(),
            P(),
            P("ctx", None),
            P("ctx", None),
            P(),
        ),
        out_specs=(P(("ctx", "pack"), None), P(("ctx", "pack"), None)),
        check_vma=False,
    )
```

profile of v0, /device:TPU:1, one launch (start us, length us, event | category | flops | bytes accessed | tf_op | source)
XLA Modules:
  0.0 515.4 jit_solution(6134942555467567787)
XLA Ops:
  7.2 1.3 copy.76
  8.6 0.9 convert_reduce_fusion
  12.8 1.5 compare_select_fusion.5
  15.1 0.9 broadcast_select_fusion
  17.6 3.5 gather_fusion
  22.0 1.8 multiply_cosine_fusion
  23.8 1.6 broadcast_compare_fusion
  25.4 22.1 %all-gather.4.cloned.1.call-done = bf16[768,2048]{1,0:T(8,128)(2,1)} async-done(((bf16[96,2048]{1,0:T(8,128)(2,1)}), bf16[768,2048]{1,0:T(8,128)(2,1)}) %all-gather.4.cloned.1.call-update) | async-done | bytes 3145744 | tf_op jit(solution)/shard_map/all_gather | solution.py:98
  47.5 7.5 %gather_fusion.2 = bf16[512,2048]{1,0:T(8,128)(2,1)} fusion(bf16[768,2048]{1,0:T(8,128)(2,1)} %all-gather.4.cloned.1.call-done, s32[1024]{0:T(1024)S(1)} %pad_clamp_fusion), kind=kCustom, calls=%fused_computation.2 | custom fusion | bytes 4196352 | tf_op jit(solution)/shard_map/gather | solution.py:105
  55.1 2.1 multiply_reduce_fusion
  57.2 2.6 fusion.34
  60.2 1.2 subtract_convert_fusion
  61.6 3.8 fusion.26
  65.4 3.9 fusion.28
  69.3 2.0 fusion.38
  71.2 89.5 %all-gather.6.cloned.1.call-done = bf16[32768,256]{1,0:T(8,128)(2,1)} async-done(((bf16[2048,256]{1,0:T(8,128)(2,1)}), bf16[32768,256]{1,0:T(8,128)(2,1)}) %all-gather.6.cloned.1.call-update) | async-done | bytes 16777232 | tf_op jit(solution)/shard_map/all_gather | solution.py:122
  160.8 24.0 %reshape.295 = bf16[16,2048,2,128]{3,2,1,0:T(2,128)(2,1)} reshape(bf16[32768,256]{1,0:T(8,128)(2,1)} %all-gather.6.cloned.1.call-done) | data formatting | bytes 33554432 | tf_op jit(solution)/shard_map/reshape | solution.py:125
  184.8 15.2 %copy.34 = bf16[16,2048,2,128]{3,1,2,0:T(8,128)(2,1)} copy(bf16[16,2048,2,128]{3,2,1,0:T(2,128)(2,1)} %reshape.295) | data formatting | bytes 33554432 | tf_op jit(solution)/shard_map/while | solution.py:139
  200.0 74.0 %all-gather.8.cloned.1.call-done = bf16[32768,256]{1,0:T(8,128)(2,1)} async-done(((bf16[2048,256]{1,0:T(8,128)(2,1)}), bf16[32768,256]{1,0:T(8,128)(2,1)}) %all-gather.8.cloned.1.call-update) | async-done | bytes 16777232 | tf_op jit(solution)/shard_map/all_gather | solution.py:123
  274.0 23.7 %reshape.296 = bf16[16,2048,2,128]{3,2,1,0:T(2,128)(2,1)} reshape(bf16[32768,256]{1,0:T(8,128)(2,1)} %all-gather.8.cloned.1.call-done) | data formatting | bytes 33554432 | tf_op jit(solution)/shard_map/reshape | solution.py:126
  297.7 15.1 %copy.35 = bf16[16,2048,2,128]{3,1,2,0:T(8,128)(2,1)} copy(bf16[16,2048,2,128]{3,2,1,0:T(2,128)(2,1)} %reshape.296) | data formatting | bytes 33554432 | tf_op jit(solution)/shard_map/while | solution.py:139
  312.8 52.8 %while.14 = (s32[]{:T(128)}, f32[2,512]{1,0:T(2,128)S(1)}, f32[2,512]{1,0:T(2,128)S(1)}, f32[512,2,128]{2,0,1:T(8,128)S(1)}, s32[16]{0:T(128)S(1)}, /*index=5*/s...) while((s32[]{:T(128)}, f32[2,512]{1,0:T(2,128)S(1)}, ...), condition=%wide.region_13.14_spmd, body=%wide.region_7.13_spmd.sunk | while | flops 1090917376 | bytes 28652856 | solution.py:139
  314.0 1.3 compare_reduce_fusion.2
  317.3 1.3 compare_reduce_fusion.2
  320.6 1.3 compare_reduce_fusion.2
  323.9 1.3 compare_reduce_fusion.2
  327.2 1.3 compare_reduce_fusion.2
  330.5 1.3 compare_reduce_fusion.2
  333.8 1.3 compare_reduce_fusion.2
  337.1 1.3 compare_reduce_fusion.2
  340.4 1.3 compare_reduce_fusion.2
  343.7 1.3 compare_reduce_fusion.2
  347.0 1.3 compare_reduce_fusion.2
  350.3 1.3 compare_reduce_fusion.2
  353.6 1.3 compare_reduce_fusion.2
  356.9 1.3 compare_reduce_fusion.2
  360.2 1.3 compare_reduce_fusion.2
  363.5 1.3 compare_reduce_fusion.2
  365.9 2.7 fusion.65
  368.7 4.1 convert_element_type.45
  372.8 1.3 fusion.44
  374.0 86.5 %reduce-scatter.3.cloned.1.call-done = f32[64,2048]{1,0:T(8,128)} async-done(((f32[512,2048]{1,0:T(8,128)}), f32[64,2048]{1,0:T(8,128)}) %reduce-scatter.3.cloned.1.call-update) | async-done | bytes 524304 | tf_op jit(solution)/shard_map/reduce_scatter | solution.py:147
  460.6 1.3 add_convert_fusion
  461.9 4.0 scatter_custom_fusion
  465.9 5.0 convert_element_type.53
  470.9 34.8 %reduce-scatter.5.cloned.1.call-done = bf16[96,2048]{1,0:T(8,128)(2,1)} async-done(((bf16[768,2048]{1,0:T(8,128)(2,1)}), bf16[96,2048]{1,0:T(8,128)(2,1)}) %reduce-scatter.5.cloned.1.call-update) | async-done | bytes 393232 | tf_op jit(solution)/shard_map/reduce_scatter | solution.py:163
  505.7 2.2 scatter_fusion
  507.9 1.0 copy-done.2
  (86 shorter events, 15.3 us)
Async XLA Ops:
  7.2 358.7 %copy-start = (bf16[256,2048]{1,0:T(8,128)(2,1)S(1)}, bf16[256,2048]{1,0:T(8,128)(2,1)}, u32[]{:S(2)}) copy-start(bf16[256,2048]{1,0:T(8,128)(2,1)} %param.18) | copy-start | bytes 3145732
  7.2 10.4 %copy-start.1 = (s32[1,512]{1,0:T(1,128)S(1)}, s32[1,512]{1,0:T(1,128)}, u32[]{:S(2)}) copy-start(s32[1,512]{1,0:T(1,128)} %param.21) | copy-start | bytes 6148
  7.2 10.4 %copy-start.6 = (s32[1,512]{1,0:T(1,128)S(1)}, s32[1,512]{1,0:T(1,128)}, u32[]{:S(2)}) copy-start(s32[1,512]{1,0:T(1,128)} %param.22) | copy-start | bytes 6148
  7.2 40.3 %all-gather.4.cloned.1.call-start = ((), (), s32[]{:S(2)}) async-start(), calls=%async_computation.2 | async-start | bytes 3538944 | tf_op jit(solution)/shard_map/all_gather | solution.py:98
  16.0 144.7 %all-gather.6.cloned.1.call-start = ((), (), s32[]{:S(2)}) async-start(), calls=%async_computation.3 | async-start | bytes 17825792 | tf_op jit(solution)/shard_map/all_gather | solution.py:122
  16.8 257.2 %all-gather.8.cloned.1.call-start = ((), (), s32[]{:S(2)}) async-start(), calls=%async_computation.4 | async-start | bytes 17825792 | tf_op jit(solution)/shard_map/all_gather | solution.py:123
  17.5 443.0 %reduce-scatter.3.cloned.1.call-start = ((), (), s32[]{:S(2)}) async-start(), calls=%async_computation.5 | async-start | bytes 4718592 | tf_op jit(solution)/shard_map/reduce_scatter | solution.py:147
  25.4 31.7 %copy-start.8 = (bf16[2048,256]{1,0:T(8,128)(2,1)S(1)}, bf16[2048,256]{1,0:T(8,128)(2,1)}, u32[]{:S(2)}) copy-start(bf16[2048,256]{1,0:T(8,128)(2,1)} %param.17) | copy-start | bytes 3145732
  25.4 31.7 %copy-start.9 = (f32[2048]{0:T(1024)S(1)}, f32[2048]{0:T(1024)}, u32[]{:S(2)}) copy-start(f32[2048]{0:T(1024)} %param.19) | copy-start | bytes 24580
  61.6 7.7 %copy-start.3 = (pred[512,2048]{1,0:T(8,128)(4,1)S(1)}, pred[512,2048]{1,0:T(8,128)(4,1)}, u32[]{:S(2)}) copy-start(pred[512,2048]{1,0:T(8,128)(4,1)} %broadcast_compare_fusion) | copy-start | bytes 3145732
  61.6 7.7 %copy-start.4 = (bf16[2048,256]{1,0:T(8,128)(2,1)S(1)}, bf16[2048,256]{1,0:T(8,128)(2,1)}, u32[]{:S(2)}) copy-start(bf16[2048,256]{1,0:T(8,128)(2,1)} %param.16) | copy-start | bytes 3145732
  365.9 6.9 %copy-start.7 = (f32[2048]{0:T(1024)S(1)}, f32[2048]{0:T(1024)}, u32[]{:S(2)}) copy-start(f32[2048]{0:T(1024)} %param.20) | copy-start | bytes 24580
  368.6 137.1 %reduce-scatter.5.cloned.1.call-start = ((), (), s32[]{:S(2)}) async-start(), calls=%async_computation.6 | async-start | bytes 3538944 | tf_op jit(solution)/shard_map/reduce_scatter | solution.py:163
  461.9 9.0 %copy-start.5 = (bf16[64,2048]{1,0:T(8,128)(2,1)}, bf16[64,2048]{1,0:T(8,128)(2,1)S(1)}, u32[]{:S(2)}) copy-start(bf16[64,2048]{1,0:T(8,128)(2,1)S(1)} %add_convert_fusion) | copy-start | bytes 786436
  507.9 1.0 copy-start.2
Sparse Core Ops, SparseCore 0:
  16.2 31.3 all-gather.3
  49.7 111.0 all-gather.5
  162.9 111.0 all-gather.7
  368.7 91.8 reduce-scatter.2
  471.0 34.6 reduce-scatter.4
where the time goes:
time: 520 us; the launch traced here: 515 us
  waiting for transfers between devices  308 us (59%)
  local copies, waits for them, and re-layouts  105 us (20%)
  other arithmetic  51.4 us (10%)
  loops' own time  21.9 us (4%)
  between operations  16 us (3%)
  matrix products  12.2 us (2%)
    all_gather x1, waiting for transfers between devices, local(): key_piece = lax.all_gather(first_keys, 'ctx', axis=0, tiled=True)  89.5 us
    reduce_scatter x1, waiting for transfers between devices, local(): lax.psum_scatter(jnp.dot(attended, w_out, preferred_element_type=jnp.floa...  86.5 us
    all_gather x1, waiting for transfers between devices, local(): value_piece = lax.all_gather(first_values, 'ctx', axis=0, tiled=True)  74 us
    reduce_scatter x1, waiting for transfers between devices, local(): lax.psum_scatter(returning.astype(jnp.bfloat16), 'pack', scatter_dimensio...  34.8 us
    while x3, local copies, waits for them, and re-layouts, local(): lax.scan(visit, running, (jnp.arange(blocks, dtype=jnp.int32), key_stack,...  30.4 us
    reshape x1, local copies, waits for them, and re-layouts, local(): key_stack = key_piece.reshape(blocks, span_len, head_count, HD)  24 us
    reshape x1, local copies, waits for them, and re-layouts, local(): value_stack = value_piece.reshape(blocks, span_len, head_count, HD)  23.7 us
    all_gather x1, waiting for transfers between devices, local(): gathered = lax.all_gather(outgoing, 'pack', axis=0, tiled=True)  22.1 us
  transfers between devices with their start and end apart: 5, of which 5 were waited for; matrix products, arithmetic and copies ran while one was open for 15% of the time, Pallas kernels for 0%

commit v1 on v0

v1 whole, which is shorter than its diff:
```python
import functools
import math

import jax
import jax.numpy as jnp
import numpy as np
from jax import lax
from jax.experimental import pallas as pl
from jax.experimental.pallas import tpu as pltpu
from jax.sharding import PartitionSpec as P

HD = 128
EPS = 1e-6
NEG = -1e30
F32 = jnp.float32
BF16 = jnp.bfloat16
MESH = pl.DeviceIdType.MESH
LOG2E = 1.4426950408889634


def turn_table():
    lane = np.arange(HD) % (HD // 2)
    turns = 10000.0 ** (-2.0 * lane / HD) / (2.0 * math.pi)
    table = np.zeros((8, HD), np.float32)
    table[0] = np.mod(turns * 128.0, 1.0)
    table[1] = turns
    table[2] = np.where(np.arange(HD) < HD // 2, -1.0, 1.0)
    return table


def cos_sin(pos, table):
    hi = jnp.floor(pos * (1.0 / 128.0))
    low = pos - hi * 128.0
    u = hi * table[0:1]
    u = u - jnp.floor(u) + low * table[1:2]
    u = u - jnp.floor(u + 0.5)
    x = u * math.pi
    y = x * x
    s = 0.0
    for n in (11, 9, 7, 5, 3):
        s = (s + (-1.0) ** ((n - 1) // 2) / math.factorial(n)) * y
    s = (s + 1.0) * x
    c = 0.0
    for n in (12, 10, 8, 6, 4, 2):
        c = (c + (-1.0) ** (n // 2) / math.factorial(n)) * y
    c = c + 1.0
    return 1.0 - 2.0 * s * s, 2.0 * s * c


def body(
    n_ctx,
    n_pack,
    hidden,
    keys,
    values,
    w_query,
    w_out,
    gain,
    router,
    routes,
    order,
    pattern,
    table,
    hidden_out,
    packed,
    rows_all,
    q_pad,
    spread,
    slot_of,
    v_ext,
    q_buf,
    o_send,
    o_in,
    st_send,
    st_in,
    acc,
    att,
    w_all,
    a_send,
    a_in,
    res,
    gate,
    row_send,
    row_recv,
    wo_send,
    wo_recv,
    q_send_sem,
    q_recv_sem,
    o_send_sem,
    o_recv_sem,
    s_send_sem,
    s_recv_sem,
    a_send_sem,
    a_recv_sem,
    loc_sem,
):
    me_c = lax.axis_index("ctx")
    me_p = lax.axis_index("pack")
    tok = hidden.shape[0]
    width = hidden.shape[1]
    span = keys.shape[0]
    routed = routes.shape[1]
    cap = rows_all.shape[1]
    per_slot = routed // n_pack
    half = cap // 2
    sib = me_p + 1 - 2 * lax.rem(me_p, 2)
    right = lax.rem(me_p + 2, n_pack)
    left = lax.rem(me_p + n_pack - 2, n_pack)
    far = lax.rem(me_p + 4, n_pack)
    sib_left = lax.rem(sib + n_pack - 2, n_pack)
    sib_right = lax.rem(sib + 2, n_pack)
    sib_far = lax.rem(sib + 4, n_pack)

    barrier = pltpu.get_barrier_semaphore()

    def greet_ctx(i, _):
        peer = lax.rem(me_c + i, n_ctx)
        pl.semaphore_signal(barrier, inc=1, device_id=(peer, me_p), device_id_type=MESH)
        return 0

    def greet_pack(i, _):
        peer = lax.rem(me_p + i, n_pack)
        pl.semaphore_signal(barrier, inc=1, device_id=(me_c, peer), device_id_type=MESH)
        return 0

    lax.fori_loop(1, n_pack, greet_pack, 0)
    lax.fori_loop(1, n_ctx, greet_ctx, 0)

    rf = routes[...].astype(F32)
    lane_i = lax.broadcasted_iota(jnp.int32, (cap, routed), 1).astype(F32)
    sub_j = lax.broadcasted_iota(jnp.int32, (cap, routed), 0).astype(F32)

    def spread_of(block):
        low = (block * tok).astype(F32)
        start = jnp.sum(jnp.where(rf < low, 1.0, 0.0), axis=1, keepdims=True)
        end = jnp.sum(jnp.where(rf < low + tok, 1.0, 0.0), axis=1, keepdims=True)
        hit = jnp.logical_and(lane_i == sub_j + start, lane_i < end)
        pos = jnp.sum(jnp.where(hit, rf + 1.0, 0.0), axis=1, keepdims=True) - 1.0
        return jnp.where(hit, 1.0, 0.0), pos

    _, my_pos = spread_of(me_p)
    lane_t = lax.broadcasted_iota(jnp.int32, (cap, tok), 1).astype(F32)
    pick = jnp.where(lane_t == my_pos - (me_p * tok).astype(F32), 1.0, 0.0).astype(BF16)
    rows_all[me_p] = jnp.dot(pick, hidden[...], preferred_element_type=F32).astype(BF16)

    pl.semaphore_wait(barrier, n_ctx + n_pack - 2)

    def row_copy(i, block, sub, peer):
        part = rows_all.at[block] if sub is None else rows_all.at[block, sub]
        return pltpu.make_async_remote_copy(
            src_ref=part,
            dst_ref=part,
            send_sem=row_send.at[i],
            recv_sem=row_recv.at[i],
            device_id=(me_c, peer),
            device_id_type=MESH,
        )

    first = pl.ds(0, half)
    second = pl.ds(half, half)
    to_right = row_copy(0, me_p, None, right)
    to_left = row_copy(1, me_p, None, left)
    to_sib = row_copy(2, me_p, None, sib)
    to_right.start()
    to_left.start()
    to_sib.start()

    own_w = pltpu.make_async_copy(w_out, w_all.at[pl.ds(me_p * tok, tok)], loc_sem)
    own_w.start()

    gain_row = gain[...]
    trig = table[...]
    base = (me_c * span).astype(F32)

    for b in range(n_pack):
        hit, _ = spread_of(jnp.int32(b))
        spread[pl.ds(b * cap, cap), :] = hit.astype(BF16)
    for h in range(2):
        v_ext[h, 0:HD, :] = jnp.transpose(values[:, h * HD : (h + 1) * HD])
        v_ext[h, HD:, :] = jnp.ones((v_ext.shape[1] - HD, span), BF16)
    order_col = jnp.transpose(jnp.broadcast_to(order[...].astype(F32), (HD, routed)))[:, 0:1]
    lane_s = lax.broadcasted_iota(jnp.int32, (routed, routed), 1).astype(F32)
    slot_of[...] = jnp.where(lane_s == order_col, 1.0, 0.0).astype(BF16)

    def project(block):
        rows = rows_all[block].astype(F32)
        mean_square = jnp.mean(rows * rows, axis=1, keepdims=True)
        normed = (rows * lax.rsqrt(mean_square + EPS) * gain_row).astype(BF16)
        proj = jnp.dot(normed, w_query[...], preferred_element_type=F32)
        _, pos = spread_of(block)
        cosine, sine = cos_sin(pos + base, trig)
        sine = sine * trig[2:3]
        start = pl.multiple_of(block * cap, cap)
        for h in range(2):
            part = proj[:, h * HD : (h + 1) * HD]
            turned = part * cosine + pltpu.roll(part, HD // 2, 1) * sine
            q_pad[pl.ds(start, cap), h * HD : (h + 1) * HD] = turned.astype(BF16)

    project(me_p)
    row_copy(0, left, None, right).wait_recv()
    fwd_right = row_copy(3, left, first, right)
    fwd_right.start()
    fwd_sib_left = row_copy(4, left, None, sib)
    fwd_sib_left.start()
    row_copy(1, right, None, left).wait_recv()
    fwd_left = row_copy(5, right, second, left)
    fwd_left.start()
    fwd_sib_right = row_copy(6, right, None, sib)
    fwd_sib_right.start()
    project(left)
    project(right)
    row_copy(2, sib, None, sib).wait_recv()
    project(sib)
    row_copy(4, sib_left, None, sib).wait_recv()
    project(sib_left)
    row_copy(6, sib_right, None, sib).wait_recv()
    project(sib_right)
    row_copy(3, far, first, right).wait_recv()
    row_copy(5, far, second, left).wait_recv()
    fwd_sib_far = row_copy(7, far, None, sib)
    fwd_sib_far.start()
    project(far)
    row_copy(7, sib_far, None, sib).wait_recv()
    project(sib_far)

    q_buf[me_c] = lax.dot_general(
        q_pad[...], spread[...], (((0,), (0,)), ((), ())), preferred_element_type=F32
    ).astype(BF16)

    def q_copy(c, k):
        return pltpu.make_async_remote_copy(
            src_ref=q_buf.at[c],
            dst_ref=q_buf.at[c],
            send_sem=q_send_sem.at[k],
            recv_sem=q_recv_sem.at[c],
            device_id=(k, me_p),
            device_id_type=MESH,
        )

    def send_q(k, _):
        q_copy(me_c, k).start()
        return 0

    lax.fori_loop(0, me_c, send_q, 0)

    w_half = tok // 2

    def w_copy(i, block, lo, size, peer):
        part = w_all.at[pl.ds(block * tok + lo, size)]
        return pltpu.make_async_remote_copy(
            src_ref=part,
            dst_ref=part,
            send_sem=wo_send.at[i],
            recv_sem=wo_recv.at[i],
            device_id=(me_c, peer),
            device_id_type=MESH,
        )

    own_w.wait()
    w_copy(0, me_p, 0, tok, right).start()
    w_copy(1, me_p, 0, tok, left).start()
    w_copy(2, me_p, 0, tok, sib).start()

    chunk = 512
    scale = LOG2E / math.sqrt(HD)
    key_iota = lax.broadcasted_iota(jnp.int32, (chunk, routed), 0).astype(F32)

    def attend(c, h, masked):
        cols = slice(h * HD, (h + 1) * HD)
        query = q_buf[c, cols, :]
        scores = []
        for i in range(span // chunk):
            s = jnp.dot(keys[i * chunk : (i + 1) * chunk, cols], query, preferred_element_type=F32)
            if masked:
                s = jnp.where(key_iota <= rf - float(i * chunk), s, NEG)
            scores.append(s)
        peak = functools.reduce(
            jnp.maximum, [jnp.max(s, axis=0, keepdims=True) for s in scores]
        )
        peak = peak * scale
        out = 0.0
        for i, s in enumerate(scores):
            weights = jnp.exp2(s * scale - peak).astype(BF16)
            out = out + jnp.dot(
                v_ext[h, :, i * chunk : (i + 1) * chunk], weights, preferred_element_type=F32
            )
        total = out[HD : HD + 1]
        return out[:HD] / total, peak + jnp.log2(total)

    for h in range(2):
        out, lse = attend(me_c, h, True)
        acc[h * HD : (h + 1) * HD, :] = out
        st_in[me_c, h : h + 1, :] = lse

    def o_copy(c, k):
        return pltpu.make_async_remote_copy(
            src_ref=o_send.at[c],
            dst_ref=o_in.at[k],
            send_sem=o_send_sem.at[c],
            recv_sem=o_recv_sem.at[k],
            device_id=(c, me_p),
            device_id_type=MESH,
        )

    def s_copy(c, k):
        return pltpu.make_async_remote_copy(
            src_ref=st_send.at[c],
            dst_ref=st_in.at[k],
            send_sem=s_send_sem.at[c],
            recv_sem=s_recv_sem.at[k],
            device_id=(c, me_p),
            device_id_type=MESH,
        )

    def serve(c, _):
        q_copy(c, me_c).wait_recv()
        st_send[c] = jnp.zeros((8, routed), F32)
        for h in range(2):
            out, lse = attend(c, h, False)
            o_send[c, h * HD : (h + 1) * HD, :] = out.astype(BF16)
            st_send[c, h : h + 1, :] = lse
        o_copy(c, me_c).start()
        s_copy(c, me_c).start()
        return 0

    cut = jnp.minimum(me_c + 1 + 5, n_ctx)
    lax.fori_loop(me_c + 1, cut, serve, 0)

    w_copy(0, left, 0, tok, right).wait_recv()
    w_copy(3, left, 0, w_half, right).start()
    w_copy(4, left, 0, tok, sib).start()
    w_copy(1, right, 0, tok, left).wait_recv()
    w_copy(5, right, w_half, w_half, left).start()
    w_copy(6, right, 0, tok, sib).start()

    lax.fori_loop(cut, n_ctx, serve, 0)

    w_copy(3, far, 0, w_half, right).wait_recv()
    w_copy(5, far, w_half, w_half, left).wait_recv()
    w_copy(7, far, 0, tok, sib).start()

    slot_rows = pl.ds(pl.multiple_of(me_p * per_slot, per_slot), per_slot)
    from_pad = lax.dot_general(
        slot_of[slot_rows, :], spread[...], (((1,), (1,)), ((), ())), preferred_element_type=F32
    ).astype(BF16)
    flat = n_pack * cap
    for n in range(0, width, 512):
        picked = 0.0
        for b in range(n_pack):
            picked = picked + jnp.dot(
                from_pad[:, b * cap : (b + 1) * cap],
                rows_all[b, :, n : n + 512],
                preferred_element_type=F32,
            )
        res[0:per_slot, n : n + 512] = picked
    res[per_slot:, :] = rows_all[me_p].astype(F32)
    gate[...] = jnp.broadcast_to(
        jax.nn.sigmoid(jnp.sum(res[...] * router[...], axis=1, keepdims=True)), gate.shape
    )

    wanted = pattern[pl.ds(me_c, 1), :]

    def merge(i, state):
        peak0, peak1, den0, den1 = state
        k = me_c - 1 - i
        o_copy(me_c, k).wait_recv()
        s_copy(me_c, k).wait_recv()
        hit = jnp.max(jnp.where(wanted == k, 1.0, 0.0), axis=1, keepdims=True)
        out = []
        for h, peak, den in ((0, peak0, den0), (1, peak1, den1)):
            rows = slice(h * HD, (h + 1) * HD)
            lse = jnp.where(hit > 0.5, st_in[k, h : h + 1, :], NEG)
            top = jnp.maximum(peak, lse)
            a = jnp.exp2(peak - top)
            b = jnp.exp2(lse - top)
            acc[rows, :] = acc[rows, :] * a + o_in[k, rows, :].astype(F32) * b
            out.append((top, den * a + b))
        return (out[0][0], out[1][0], out[0][1], out[1][1])

    ones = jnp.ones((1, routed), F32)
    _, _, den0, den1 = lax.fori_loop(
        0, me_c, merge, (st_in[me_c, 0:1, :], st_in[me_c, 1:2, :], ones, ones)
    )
    att[0:HD, :] = (acc[0:HD, :] / den0).astype(BF16)
    att[HD:, :] = (acc[HD:, :] / den1).astype(BF16)

    by_slot = lax.dot_general(
        slot_of[...], att[...], (((1,), (1,)), ((), ())), preferred_element_type=F32
    ).astype(BF16)
    by_owner = lax.dot_general(
        spread[...], att[...], (((1,), (1,)), ((), ())), preferred_element_type=F32
    ).astype(BF16)
    for d in range(n_pack):
        a_send[d, 0:per_slot, :] = by_slot[d * per_slot : (d + 1) * per_slot]
        a_send[d, per_slot:, :] = by_owner[d * cap : (d + 1) * cap]

    def a_copy(src, dst):
        return pltpu.make_async_remote_copy(
            src_ref=a_send.at[dst],
            dst_ref=a_in.at[src],
            send_sem=a_send_sem.at[dst],
            recv_sem=a_recv_sem.at[src],
            device_id=(me_c, dst),
            device_id_type=MESH,
        )

    def send_a(i, _):
        a_copy(me_p, lax.rem(me_p + i, n_pack)).start()
        return 0

    lax.fori_loop(1, n_pack, send_a, 0)
    a_in[me_p] = a_send[me_p]

    w_copy(2, sib, 0, tok, sib).wait_recv()
    w_copy(4, sib_left, 0, tok, sib).wait_recv()
    w_copy(6, sib_right, 0, tok, sib).wait_recv()
    w_copy(7, sib_far, 0, tok, sib).wait_recv()

    def take_a(i, _):
        peer = lax.rem(me_p + i, n_pack)
        a_copy(peer, me_p).wait_recv()
        return 0

    lax.fori_loop(1, n_pack, take_a, 0)

    present = lax.dot_general(
        pick, jnp.ones((cap, HD), BF16), (((0,), (0,)), ((), ())), preferred_element_type=F32
    )[:, 0:1]
    for n in range(0, width, 512):
        cols = slice(n, n + 512)
        mixed = 0.0
        for b in range(n_pack):
            mixed = mixed + jnp.dot(
                a_in[b], w_all[b * tok : (b + 1) * tok, cols], preferred_element_type=F32
            )
        updated = (res[:, cols] + gate[:, 0:1] * mixed).astype(BF16)
        packed[:, cols] = updated[0:per_slot]
        placed = lax.dot_general(
            pick, updated[per_slot:], (((0,), (0,)), ((), ())), preferred_element_type=F32
        )
        hidden_out[:, cols] = jnp.where(present > 0.5, placed.astype(BF16), hidden[:, cols])

    to_right.wait_send()
    to_left.wait_send()
    to_sib.wait_send()
    fwd_right.wait_send()
    fwd_left.wait_send()
    fwd_sib_left.wait_send()
    fwd_sib_right.wait_send()
    fwd_sib_far.wait_send()
    w_copy(0, me_p, 0, tok, right).wait_send()
    w_copy(1, me_p, 0, tok, left).wait_send()
    w_copy(2, me_p, 0, tok, sib).wait_send()
    w_copy(3, left, 0, w_half, right).wait_send()
    w_copy(4, left, 0, tok, sib).wait_send()
    w_copy(5, right, w_half, w_half, left).wait_send()
    w_copy(6, right, 0, tok, sib).wait_send()
    w_copy(7, far, 0, tok, sib).wait_send()

    def sent_q(k, _):
        q_copy(me_c, k).wait_send()
        return 0

    lax.fori_loop(0, me_c, sent_q, 0)

    def sent_o(c, _):
        o_copy(c, me_c).wait_send()
        s_copy(c, me_c).wait_send()
        return 0

    lax.fori_loop(me_c + 1, n_ctx, sent_o, 0)

    def sent_a(i, _):
        a_copy(me_p, lax.rem(me_p + i, n_pack)).wait_send()
        return 0

    lax.fori_loop(1, n_pack, sent_a, 0)


def local(n_ctx, n_pack, *args):
    hidden, keys, values, w_query, w_out, gain, router, routes, order, pattern = args
    tok, width = hidden.shape
    span, heads = keys.shape
    routed = routes.shape[1]
    cap = 3 * tok // 8
    per_slot = routed // n_pack
    both = per_slot + cap
    vmem = pl.BlockSpec(memory_space=pltpu.VMEM)
    dma = pltpu.SemaphoreType.DMA
    return pl.pallas_call(
        functools.partial(body, n_ctx, n_pack),
        out_shape=(
            jax.ShapeDtypeStruct((tok, width), BF16),
            jax.ShapeDtypeStruct((per_slot, width), BF16),
        ),
        in_specs=[vmem] * 11,
        out_specs=(vmem, vmem),
        scratch_shapes=[
            pltpu.VMEM((n_pack, cap, width), BF16),
            pltpu.VMEM((n_pack * cap, heads), BF16),
            pltpu.VMEM((n_pack * cap, routed), BF16),
            pltpu.VMEM((routed, routed), BF16),
            pltpu.VMEM((2, HD + 16, span), BF16),
            pltpu.VMEM((n_ctx, heads, routed), BF16),
            pltpu.VMEM((n_ctx, heads, routed), BF16),
            pltpu.VMEM((n_ctx, heads, routed), BF16),
            pltpu.VMEM((n_ctx, 8, routed), F32),
            pltpu.VMEM((n_ctx, 8, routed), F32),
            pltpu.VMEM((heads, routed), F32),
            pltpu.VMEM((heads, routed), BF16),
            pltpu.VMEM((n_pack * tok, width), BF16),
            pltpu.VMEM((n_pack, both, heads), BF16),
            pltpu.VMEM((n_pack, both, heads), BF16),
            pltpu.VMEM((both, width), F32),
            pltpu.VMEM((both, HD), F32),
            dma((8,)),
            dma((8,)),
            dma((8,)),
            dma((8,)),
            dma((n_ctx,)),
            dma((n_ctx,)),
            dma((n_ctx,)),
            dma((n_ctx,)),
            dma((n_ctx,)),
            dma((n_ctx,)),
            dma((n_pack,)),
            dma((n_pack,)),
            dma,
        ],
        compiler_params=pltpu.CompilerParams(
            collective_id=0, has_side_effects=True, vmem_limit_bytes=60 << 20
        ),
        name="routed_attention",
    )(
        hidden,
        keys,
        values,
        w_query,
        w_out,
        gain.reshape(1, width),
        router.reshape(1, width),
        routes,
        order,
        pattern,
        jnp.asarray(turn_table()),
    )


def solution(mesh):
    return jax.shard_map(
        functools.partial(local, mesh.shape["ctx"], mesh.shape["pack"]),
        mesh=mesh,
        in_specs=(
            P(("ctx", "pack"), None),
            P("ctx", "pack"),
            P("ctx", "pack"),
            P(None, "pack"),
            P("pack", None),
            P(),
            P(),
            P("ctx", None),
            P("ctx", None),
            P(),
        ),
        out_specs=(P(("ctx", "pack"), None), P(("ctx", "pack"), None)),
        check_vma=False,
    )
```

time: 520 us -> 169 us (0.33)
  the two profiles are of different devices: /device:TPU:1 before, /device:TPU:121 now
where the time goes in v1:
time: 169 us
  Pallas kernels  165 us (98%)
  local copies, waits for them, and re-layouts  3.05 us (2%)
    pallas_call x1, Pallas kernels, local(): pl.pallas_call(functools.partial(body, n_ctx, n_pack), out_shape=(jax.Sha...  165 us

profile of v1, /device:TPU:121, one launch (start us, length us, event | category | flops | bytes accessed | tf_op | source)
XLA Modules:
  0.0 168.7 jit_solution(17995678082868963559)
XLA Ops:
  0.6 165.0 %routed_attention.1 = (bf16[256,2048]{1,0:T(8,128)(2,1)}, bf16[64,2048]{1,0:T(8,128)(2,1)}) custom-call(bf16[256,2048]{1,0:T(8,128)(2,1)} %hidden.1, bf16[2048,256]{1,0:T(8,128)(2,1)} %keys.1, bf16[2048,256]{1,0:T(8,128)(2,1)} %values.1, bf16[2048,256]{1,0:T(8,128)(2,1)} %w_query.1, bf16[256,2048]{1,0:T(8,128)(2,1)} %w_out.1, f32[1,2048]{1,0:T(1,128)} %bitcast.2, ...), custom_call_target="tpu_custom_call" | custom-call | tf_op jit(solution)/shard_map/routed_attention/pallas_call | solution.py:490
  165.7 0.0 copy-start
  165.7 2.3 %copy.15 = bf16[256,2048]{1,0:T(8,128)(2,1)} copy(bf16[256,2048]{1,0:T(8,128)(2,1)} %get-tuple-element.4) | data formatting | bytes 2097152
  168.0 0.0 copy-done
  168.0 0.7 copy.16
Async XLA Ops:
  165.7 2.4 %copy-start = (bf16[64,2048]{1,0:T(8,128)(2,1)S(1)}, bf16[64,2048]{1,0:T(8,128)(2,1)}, u32[]{:S(2)}) copy-start(bf16[64,2048]{1,0:T(8,128)(2,1)} %get-tuple-element.5) | copy-start | bytes 786436

commit v2 on v1

--- a/solution.py
+++ b/solution.py
@@ -67,12 +67,15 @@
     q_pad,
     spread,
     slot_of,
-    v_ext,
+    kbuf,
+    vbuf,
     q_buf,
     o_send,
     o_in,
     st_send,
     st_in,
+    own,
+    own_st,
     acc,
     att,
     w_all,
@@ -84,6 +87,8 @@
     row_recv,
     wo_send,
     wo_recv,
+    kv_send,
+    kv_recv,
     q_send_sem,
     q_recv_sem,
     o_send_sem,
@@ -113,18 +118,31 @@
 
     barrier = pltpu.get_barrier_semaphore()
 
+    side = math.isqrt(n_ctx)
+    y = me_c // side
+    z = lax.rem(me_c, side)
+    core = lax.rem(me_p, 2)
+
+    def along_z(step):
+        return y * side + lax.rem(z + step, side)
+
+    def along_y(step):
+        return lax.rem(y + step, side) * side + z
+
+    def greet(c, p):
+        pl.semaphore_signal(barrier, inc=1, device_id=(c, p), device_id_type=MESH)
+
+    def greet_pack(i, _):
+        greet(me_c, lax.rem(me_p + i, n_pack))
+        return 0
+
     def greet_ctx(i, _):
-        peer = lax.rem(me_c + i, n_ctx)
-        pl.semaphore_signal(barrier, inc=1, device_id=(peer, me_p), device_id_type=MESH)
-        return 0
-
-    def greet_pack(i, _):
-        peer = lax.rem(me_p + i, n_pack)
-        pl.semaphore_signal(barrier, inc=1, device_id=(me_c, peer), device_id_type=MESH)
+        greet(along_y(i), me_p)
+        greet(along_z(i), me_p)
         return 0
 
     lax.fori_loop(1, n_pack, greet_pack, 0)
-    lax.fori_loop(1, n_ctx, greet_ctx, 0)
+    lax.fori_loop(1, side, greet_ctx, 0)
 
     rf = routes[...].astype(F32)
     lane_i = lax.broadcasted_iota(jnp.int32, (cap, routed), 1).astype(F32)
@@ -143,7 +161,7 @@
     pick = jnp.where(lane_t == my_pos - (me_p * tok).astype(F32), 1.0, 0.0).astype(BF16)
     rows_all[me_p] = jnp.dot(pick, hidden[...], preferred_element_type=F32).astype(BF16)
 
-    pl.semaphore_wait(barrier, n_ctx + n_pack - 2)
+    pl.semaphore_wait(barrier, 2 * (side - 1) + n_pack - 1)
 
     def row_copy(i, block, sub, peer):
         part = rows_all.at[block] if sub is None else rows_all.at[block, sub]
@@ -165,6 +183,47 @@
     to_left.start()
     to_sib.start()
 
+    key_ring = (along_y, along_z)
+    key_at = (y, z)
+    ahead = 1 + 2 * core
+    behind = side - ahead
+
+    def k_copy(h, j, i, step):
+        part = kbuf.at[h, j]
+        return pltpu.make_async_remote_copy(
+            src_ref=part,
+            dst_ref=part,
+            send_sem=kv_send.at[h * 3 + i],
+            recv_sem=kv_recv.at[h * side + j],
+            device_id=(key_ring[h](step), me_p),
+            device_id_type=MESH,
+        )
+
+    def v_copy(h, j, i, step):
+        part = vbuf.at[h, j, 0:HD]
+        return pltpu.make_async_remote_copy(
+            src_ref=part,
+            dst_ref=part,
+            send_sem=kv_send.at[6 + h * 3 + i],
+            recv_sem=kv_recv.at[2 * side + h * side + j],
+            device_id=(key_ring[h](step), me_p),
+            device_id_type=MESH,
+        )
+
+    for h in range(2):
+        kbuf[h, key_at[h]] = keys[:, h * HD : (h + 1) * HD]
+        k_copy(h, key_at[h], 0, 1).start()
+        k_copy(h, key_at[h], 1, side - 1).start()
+    for h in range(2):
+        vbuf[h, key_at[h], 0:HD, :] = jnp.transpose(values[:, h * HD : (h + 1) * HD])
+        v_copy(h, key_at[h], 0, 1).start()
+        v_copy(h, key_at[h], 1, side - 1).start()
+        for j in range(side):
+            vbuf[h, j, HD:, :] = jnp.ones((vbuf.shape[2] - HD, span), BF16)
+
+    def key_block(h, step):
+        return lax.rem(key_at[h] + step, side)
+
     own_w = pltpu.make_async_copy(w_out, w_all.at[pl.ds(me_p * tok, tok)], loc_sem)
     own_w.start()
 
@@ -175,9 +234,6 @@
     for b in range(n_pack):
         hit, _ = spread_of(jnp.int32(b))
         spread[pl.ds(b * cap, cap), :] = hit.astype(BF16)
-    for h in range(2):
-        v_ext[h, 0:HD, :] = jnp.transpose(values[:, h * HD : (h + 1) * HD])
-        v_ext[h, HD:, :] = jnp.ones((v_ext.shape[1] - HD, span), BF16)
     order_col = jnp.transpose(jnp.broadcast_to(order[...].astype(F32), (HD, routed)))[:, 0:1]
     lane_s = lax.broadcasted_iota(jnp.int32, (routed, routed), 1).astype(F32)
     slot_of[...] = jnp.where(lane_s == order_col, 1.0, 0.0).astype(BF16)
@@ -209,6 +265,9 @@
     fwd_sib_right.start()
     project(left)
     project(right)
+    for h in range(2):
+        k_copy(h, key_block(h, behind), 0, behind).wait_recv()
+        k_copy(h, key_block(h, behind), 2, ahead).start()
     row_copy(2, sib, None, sib).wait_recv()
     project(sib)
     row_copy(4, sib_left, None, sib).wait_recv()
@@ -223,25 +282,30 @@
     row_copy(7, sib_far, None, sib).wait_recv()
     project(sib_far)
 
-    q_buf[me_c] = lax.dot_general(
+    query = lax.dot_general(
         q_pad[...], spread[...], (((0,), (0,)), ((), ())), preferred_element_type=F32
     ).astype(BF16)
-
-    def q_copy(c, k):
-        return pltpu.make_async_remote_copy(
-            src_ref=q_buf.at[c],
-            dst_ref=q_buf.at[c],
-            send_sem=q_send_sem.at[k],
-            recv_sem=q_recv_sem.at[c],
-            device_id=(k, me_p),
-            device_id_type=MESH,
-        )
-
-    def send_q(k, _):
-        q_copy(me_c, k).start()
-        return 0
-
-    lax.fori_loop(0, me_c, send_q, 0)
+    q_buf[0, z] = query[0:HD]
+    q_buf[1, y] = query[HD:]
+    q_ring = (along_z, along_y)
+    q_at = (z, y)
+
+    def q_copy(h, src, step):
+        return pltpu.make_async_remote_copy(
+            src_ref=q_buf.at[h, src],
+            dst_ref=q_buf.at[h, src],
+            send_sem=q_send_sem.at[h * side + step],
+            recv_sem=q_recv_sem.at[h * side + src],
+            device_id=(q_ring[h](step), me_p),
+            device_id_type=MESH,
+        )
+
+    for step in (1, 3, 2):
+        for h in range(2):
+            q_copy(h, q_at[h], step).start()
+    for h in range(2):
+        v_copy(h, key_block(h, behind), 0, behind).wait_recv()
+        v_copy(h, key_block(h, behind), 2, ahead).start()
 
     w_half = tok // 2
 
@@ -265,12 +329,13 @@
     scale = LOG2E / math.sqrt(HD)
     key_iota = lax.broadcasted_iota(jnp.int32, (chunk, routed), 0).astype(F32)
 
-    def attend(c, h, masked):
-        cols = slice(h * HD, (h + 1) * HD)
-        query = q_buf[c, cols, :]
+    def attend(h, t, j, masked):
+        query = q_buf[h, t]
         scores = []
         for i in range(span // chunk):
-            s = jnp.dot(keys[i * chunk : (i + 1) * chunk, cols], query, preferred_element_type=F32)
+            s = jnp.dot(
+                kbuf[h, j, i * chunk : (i + 1) * chunk, :], query, preferred_element_type=F32
+            )
             if masked:
                 s = jnp.where(key_iota <= rf - float(i * chunk), s, NEG)
             scores.append(s)
@@ -282,49 +347,109 @@
         for i, s in enumerate(scores):
             weights = jnp.exp2(s * scale - peak).astype(BF16)
             out = out + jnp.dot(
-                v_ext[h, :, i * chunk : (i + 1) * chunk], weights, preferred_element_type=F32
+                vbuf[h, j, :, i * chunk : (i + 1) * chunk], weights, preferred_element_type=F32
             )
         total = out[HD : HD + 1]
         return out[:HD] / total, peak + jnp.log2(total)
 
+    def less(a, b):
+        return (b - a + side - 1) // side
+
+    def same(a, b):
+        return 1 - less(a, b) - less(b, a)
+
+    def blend(h, one, two):
+        return one + h * (two - one)
+
+    def visit(h, t, peak, den):
+        count = blend(h, y + less(z, t), side * less(y, t) + z * same(y, t))
+        span_q = blend(h, y * side + t, t * side + z)
+        wanted = pattern[pl.ds(span_q, 1), :]
+
+        def one(j, state):
+            peak, den = state
+            span_k = blend(h, j * side + z, y * side + j)
+            hit = jnp.max(jnp.where(wanted == span_k, 1.0, 0.0), axis=1, keepdims=True)
+            out, lse = attend(h, t, j, False)
+            lse = jnp.where(hit > 0.5, lse, NEG)
+            top = jnp.maximum(peak, lse)
+            a = jnp.exp2(peak - top)
+            b = jnp.exp2(lse - top) * hit
+            acc[...] = acc[...] * a + out * b
+            return top, den * a + b
+
+        return lax.fori_loop(0, count, one, (peak, den))
+
+    def begin(h, _):
+        out, lse = attend(h, blend(h, z, y), blend(h, y, z), True)
+        own[h] = out
+        own_st[h, 0:1, :] = lse
+        return 0
+
+    lax.fori_loop(0, 2, begin, 0)
+
     for h in range(2):
-        out, lse = attend(me_c, h, True)
-        acc[h * HD : (h + 1) * HD, :] = out
-        st_in[me_c, h : h + 1, :] = lse
-
-    def o_copy(c, k):
-        return pltpu.make_async_remote_copy(
-            src_ref=o_send.at[c],
-            dst_ref=o_in.at[k],
-            send_sem=o_send_sem.at[c],
-            recv_sem=o_recv_sem.at[k],
-            device_id=(c, me_p),
-            device_id_type=MESH,
-        )
-
-    def s_copy(c, k):
-        return pltpu.make_async_remote_copy(
-            src_ref=st_send.at[c],
-            dst_ref=st_in.at[k],
-            send_sem=s_send_sem.at[c],
-            recv_sem=s_recv_sem.at[k],
-            device_id=(c, me_p),
-            device_id_type=MESH,
-        )
-
-    def serve(c, _):
-        q_copy(c, me_c).wait_recv()
-        st_send[c] = jnp.zeros((8, routed), F32)
-        for h in range(2):
-            out, lse = attend(c, h, False)
-            o_send[c, h * HD : (h + 1) * HD, :] = out.astype(BF16)
-            st_send[c, h : h + 1, :] = lse
-        o_copy(c, me_c).start()
-        s_copy(c, me_c).start()
-        return 0
-
-    cut = jnp.minimum(me_c + 1 + 5, n_ctx)
-    lax.fori_loop(me_c + 1, cut, serve, 0)
+        k_copy(h, key_block(h, ahead), 0, ahead).wait_recv()
+        v_copy(h, key_block(h, ahead), 0, ahead).wait_recv()
+        k_copy(h, key_block(h, 2), 0, behind).wait_recv()
+        v_copy(h, key_block(h, 2), 0, behind).wait_recv()
+
+    ones = jnp.ones((1, routed), F32)
+
+    def finish_own(h, _):
+        acc[...] = own[h]
+        peak, den = visit(h, blend(h, z, y), own_st[h, 0:1, :], ones)
+        own[h] = acc[...]
+        own_st[h, 0:1, :] = peak
+        own_st[h, 1:2, :] = den
+        return 0
+
+    lax.fori_loop(0, 2, finish_own, 0)
+
+    def o_copy(h, src, dst):
+        return pltpu.make_async_remote_copy(
+            src_ref=o_send.at[h, dst],
+            dst_ref=o_in.at[h, src],
+            send_sem=o_send_sem.at[h * side + dst],
+            recv_sem=o_recv_sem.at[h * side + src],
+            device_id=(blend(h, y * side + dst, dst * side + z), me_p),
+            device_id_type=MESH,
+        )
+
+    def s_copy(h, src, dst):
+        return pltpu.make_async_remote_copy(
+            src_ref=st_send.at[h, dst],
+            dst_ref=st_in.at[h, src],
+            send_sem=s_send_sem.at[h * side + dst],
+            recv_sem=s_recv_sem.at[h * side + src],
+            device_id=(blend(h, y * side + dst, dst * side + z), me_p),
+            device_id_type=MESH,
+        )
+
+    def serve(i, _):
+        step = i // 2
+        h = lax.rem(i, 2)
+        at = blend(h, z, y)
+        t = lax.rem(at + step, side)
+        pltpu.make_async_remote_copy(
+            src_ref=q_buf.at[h, t],
+            dst_ref=q_buf.at[h, t],
+            send_sem=q_send_sem.at[h * side + step],
+            recv_sem=q_recv_sem.at[h * side + t],
+            device_id=(blend(h, along_z(step), along_y(step)), me_p),
+            device_id_type=MESH,
+        ).wait_recv()
+        acc[...] = jnp.zeros((HD, routed), F32)
+        peak, den = visit(h, t, ones * NEG, ones * 0.0)
+        o_send[h, t] = (acc[...] / jnp.where(den > 0.0, den, 1.0)).astype(BF16)
+        st_send[h, t] = jnp.broadcast_to(
+            jnp.where(den > 0.0, peak + jnp.log2(den), NEG), (8, routed)
+        )
+        o_copy(h, at, t).start()
+        s_copy(h, at, t).start()
+        return 0
+
+    lax.fori_loop(2, 6, serve, 0)
 
     w_copy(0, left, 0, tok, right).wait_recv()
     w_copy(3, left, 0, w_half, right).start()
@@ -333,7 +458,7 @@
     w_copy(5, right, w_half, w_half, left).start()
     w_copy(6, right, 0, tok, sib).start()
 
-    lax.fori_loop(cut, n_ctx, serve, 0)
+    lax.fori_loop(6, 2 * side, serve, 0)
 
     w_copy(3, far, 0, w_half, right).wait_recv()
     w_copy(5, far, w_half, w_half, left).wait_recv()
@@ -358,31 +483,20 @@
         jax.nn.sigmoid(jnp.sum(res[...] * router[...], axis=1, keepdims=True)), gate.shape
     )
 
-    wanted = pattern[pl.ds(me_c, 1), :]
-
-    def merge(i, state):
-        peak0, peak1, den0, den1 = state
-        k = me_c - 1 - i
-        o_copy(me_c, k).wait_recv()
-        s_copy(me_c, k).wait_recv()
-        hit = jnp.max(jnp.where(wanted == k, 1.0, 0.0), axis=1, keepdims=True)
-        out = []
-        for h, peak, den in ((0, peak0, den0), (1, peak1, den1)):
-            rows = slice(h * HD, (h + 1) * HD)
-            lse = jnp.where(hit > 0.5, st_in[k, h : h + 1, :], NEG)
+    for h in range(2):
+        peak, den = own_st[h, 0:1, :], own_st[h, 1:2, :]
+        total = own[h]
+        for step in (3, 2, 1):
+            src = lax.rem(q_at[h] + step, side)
+            o_copy(h, src, q_at[h]).wait_recv()
+            s_copy(h, src, q_at[h]).wait_recv()
+            lse = st_in[h, src, 0:1, :]
             top = jnp.maximum(peak, lse)
             a = jnp.exp2(peak - top)
             b = jnp.exp2(lse - top)
-            acc[rows, :] = acc[rows, :] * a + o_in[k, rows, :].astype(F32) * b
-            out.append((top, den * a + b))
-        return (out[0][0], out[1][0], out[0][1], out[1][1])
-
-    ones = jnp.ones((1, routed), F32)
-    _, _, den0, den1 = lax.fori_loop(
-        0, me_c, merge, (st_in[me_c, 0:1, :], st_in[me_c, 1:2, :], ones, ones)
-    )
-    att[0:HD, :] = (acc[0:HD, :] / den0).astype(BF16)
-    att[HD:, :] = (acc[HD:, :] / den1).astype(BF16)
+            total = total * a + o_in[h, src].astype(F32) * b
+            peak, den = top, den * a + b
+        att[h * HD : (h + 1) * HD, :] = (total / den).astype(BF16)
 
     by_slot = lax.dot_general(
         slot_of[...], att[...], (((1,), (1,)), ((), ())), preferred_element_type=F32
@@ -457,18 +571,18 @@
     w_copy(6, right, 0, tok, sib).wait_send()
     w_copy(7, far, 0, tok, sib).wait_send()
 
-    def sent_q(k, _):
-        q_copy(me_c, k).wait_send()
-        return 0
-
-    lax.fori_loop(0, me_c, sent_q, 0)
-
-    def sent_o(c, _):
-        o_copy(c, me_c).wait_send()
-        s_copy(c, me_c).wait_send()
-        return 0
-
-    lax.fori_loop(me_c + 1, n_ctx, sent_o, 0)
+    for h in range(2):
+        k_copy(h, key_at[h], 0, 1).wait_send()
+        k_copy(h, key_at[h], 1, side - 1).wait_send()
+        k_copy(h, key_block(h, behind), 2, ahead).wait_send()
+        v_copy(h, key_at[h], 0, 1).wait_send()
+        v_copy(h, key_at[h], 1, side - 1).wait_send()
+        v_copy(h, key_block(h, behind), 2, ahead).wait_send()
+        for step in (1, 2, 3):
+            dst = lax.rem(q_at[h] + step, side)
+            q_copy(h, q_at[h], step).wait_send()
+            o_copy(h, q_at[h], dst).wait_send()
+            s_copy(h, q_at[h], dst).wait_send()
 
     def sent_a(i, _):
         a_copy(me_p, lax.rem(me_p + i, n_pack)).wait_send()
@@ -485,6 +599,7 @@
     cap = 3 * tok // 8
     per_slot = routed // n_pack
     both = per_slot + cap
+    side = math.isqrt(n_ctx)
     vmem = pl.BlockSpec(memory_space=pltpu.VMEM)
     dma = pltpu.SemaphoreType.DMA
     return pl.pallas_call(
@@ -500,13 +615,16 @@
             pltpu.VMEM((n_pack * cap, heads), BF16),
             pltpu.VMEM((n_pack * cap, routed), BF16),
             pltpu.VMEM((routed, routed), BF16),
-            pltpu.VMEM((2, HD + 16, span), BF16),
-            pltpu.VMEM((n_ctx, heads, routed), BF16),
-            pltpu.VMEM((n_ctx, heads, routed), BF16),
-            pltpu.VMEM((n_ctx, heads, routed), BF16),
-            pltpu.VMEM((n_ctx, 8, routed), F32),
-            pltpu.VMEM((n_ctx, 8, routed), F32),
-            pltpu.VMEM((heads, routed), F32),
+            pltpu.VMEM((2, side, span, HD), BF16),
+            pltpu.VMEM((2, side, HD + 16, span), BF16),
+            pltpu.VMEM((2, side, HD, routed), BF16),
+            pltpu.VMEM((2, side, HD, routed), BF16),
+            pltpu.VMEM((2, side, HD, routed), BF16),
+            pltpu.VMEM((2, side, 8, routed), F32),
+            pltpu.VMEM((2, side, 8, routed), F32),
+            pltpu.VMEM((2, HD, routed), F32),
+            pltpu.VMEM((2, 8, routed), F32),
+            pltpu.VMEM((HD, routed), F32),
             pltpu.VMEM((heads, routed), BF16),
             pltpu.VMEM((n_pack * tok, width), BF16),
             pltpu.VMEM((n_pack, both, heads), BF16),
@@ -517,12 +635,14 @@
             dma((8,)),
             dma((8,)),
             dma((8,)),
-            dma((n_ctx,)),
-            dma((n_ctx,)),
-            dma((n_ctx,)),
-            dma((n_ctx,)),
-            dma((n_ctx,)),
-            dma((n_ctx,)),
+            dma((12,)),
+            dma((4 * side,)),
+            dma((2 * side,)),
+            dma((2 * side,)),
+            dma((2 * side,)),
+            dma((2 * side,)),
+            dma((2 * side,)),
+            dma((2 * side,)),
             dma((n_pack,)),
             dma((n_pack,)),
             dma,

time: 169 us -> 109 us (0.64)
  the two profiles are of different devices: /device:TPU:121 before, /device:TPU:41 now
where the time goes in v2:
time: 109 us
  Pallas kernels  105 us (96%)
  local copies, waits for them, and re-layouts  3.05 us (3%)
    pallas_call x1, Pallas kernels, local(): pl.pallas_call(functools.partial(body, n_ctx, n_pack), out_shape=(jax.Sha...  105 us
    unnamed x4, local copies, waits for them, and re-layouts  3.05 us

profile of v2, /device:TPU:41, one launch (start us, length us, event | category | flops | bytes accessed | tf_op | source)
XLA Modules:
  0.0 109.0 jit_solution(3132033616876328447)
XLA Ops:
  0.6 105.3 %routed_attention.1 = (bf16[256,2048]{1,0:T(8,128)(2,1)}, bf16[64,2048]{1,0:T(8,128)(2,1)}) custom-call(bf16[256,2048]{1,0:T(8,128)(2,1)} %hidden.1, bf16[2048,256]{1,0:T(8,128)(2,1)} %keys.1, bf16[2048,256]{1,0:T(8,128)(2,1)} %values.1, bf16[2048,256]{1,0:T(8,128)(2,1)} %w_query.1, bf16[256,2048]{1,0:T(8,128)(2,1)} %w_out.1, f32[1,2048]{1,0:T(1,128)} %bitcast.2, ...), custom_call_target="tpu_custom_call" | custom-call | tf_op jit(solution)/shard_map/routed_attention/pallas_call | solution.py:605
  105.9 0.0 copy-start
  105.9 2.3 %copy.15 = bf16[256,2048]{1,0:T(8,128)(2,1)} copy(bf16[256,2048]{1,0:T(8,128)(2,1)} %get-tuple-element.4) | data formatting | bytes 2097152
  108.3 0.0 copy-done
  108.3 0.7 copy.16
Async XLA Ops:
  105.9 2.4 %copy-start = (bf16[64,2048]{1,0:T(8,128)(2,1)S(1)}, bf16[64,2048]{1,0:T(8,128)(2,1)}, u32[]{:S(2)}) copy-start(bf16[64,2048]{1,0:T(8,128)(2,1)} %get-tuple-element.5) | copy-start | bytes 786436

commit v3 on v2

--- a/solution.py
+++ b/solution.py
@@ -66,7 +66,9 @@
     rows_all,
     q_pad,
     spread,
+    gather,
     slot_of,
+    pos_col,
     kbuf,
     vbuf,
     q_buf,
@@ -74,9 +76,8 @@
     o_in,
     st_send,
     st_in,
-    own,
-    own_st,
     acc,
+    state,
     att,
     w_all,
     a_send,
@@ -200,7 +201,7 @@
         )
 
     def v_copy(h, j, i, step):
-        part = vbuf.at[h, j, 0:HD]
+        part = vbuf.at[h, j, :, pl.ds(0, HD)]
         return pltpu.make_async_remote_copy(
             src_ref=part,
             dst_ref=part,
@@ -215,11 +216,12 @@
         k_copy(h, key_at[h], 0, 1).start()
         k_copy(h, key_at[h], 1, side - 1).start()
     for h in range(2):
-        vbuf[h, key_at[h], 0:HD, :] = jnp.transpose(values[:, h * HD : (h + 1) * HD])
+        vbuf[h, key_at[h], :, 0:HD] = values[:, h * HD : (h + 1) * HD]
         v_copy(h, key_at[h], 0, 1).start()
         v_copy(h, key_at[h], 1, side - 1).start()
+    for h in range(2):
         for j in range(side):
-            vbuf[h, j, HD:, :] = jnp.ones((vbuf.shape[2] - HD, span), BF16)
+            vbuf[h, j, :, HD:] = jnp.ones((span, HD), BF16)
 
     def key_block(h, step):
         return lax.rem(key_at[h] + step, side)
@@ -234,6 +236,21 @@
     for b in range(n_pack):
         hit, _ = spread_of(jnp.int32(b))
         spread[pl.ds(b * cap, cap), :] = hit.astype(BF16)
+    flat = n_pack * cap
+    lane_f = lax.broadcasted_iota(jnp.int32, (1, flat), 1).astype(F32)
+    start_f = lane_f * 0.0
+    end_f = lane_f * 0.0
+    for b in range(n_pack):
+        inside = jnp.logical_and(lane_f >= b * cap, lane_f < (b + 1) * cap)
+        start = jnp.sum(jnp.where(rf < b * tok, 1.0, 0.0), axis=1, keepdims=True)
+        end = jnp.sum(jnp.where(rf < (b + 1) * tok, 1.0, 0.0), axis=1, keepdims=True)
+        start_f = jnp.where(inside, start + lane_f - b * cap, start_f)
+        end_f = jnp.where(inside, end, end_f)
+    row_i = lax.broadcasted_iota(jnp.int32, (routed, flat), 0).astype(F32)
+    gather[...] = jnp.where(
+        jnp.logical_and(row_i == start_f, row_i < end_f), 1.0, 0.0
+    ).astype(BF16)
+    pos_col[...] = jnp.transpose(jnp.broadcast_to(rf, (HD, routed)))
     order_col = jnp.transpose(jnp.broadcast_to(order[...].astype(F32), (HD, routed)))[:, 0:1]
     lane_s = lax.broadcasted_iota(jnp.int32, (routed, routed), 1).astype(F32)
     slot_of[...] = jnp.where(lane_s == order_col, 1.0, 0.0).astype(BF16)
@@ -278,35 +295,6 @@
     row_copy(5, far, second, left).wait_recv()
     fwd_sib_far = row_copy(7, far, None, sib)
     fwd_sib_far.start()
-    project(far)
-    row_copy(7, sib_far, None, sib).wait_recv()
-    project(sib_far)
-
-    query = lax.dot_general(
-        q_pad[...], spread[...], (((0,), (0,)), ((), ())), preferred_element_type=F32
-    ).astype(BF16)
-    q_buf[0, z] = query[0:HD]
-    q_buf[1, y] = query[HD:]
-    q_ring = (along_z, along_y)
-    q_at = (z, y)
-
-    def q_copy(h, src, step):
-        return pltpu.make_async_remote_copy(
-            src_ref=q_buf.at[h, src],
-            dst_ref=q_buf.at[h, src],
-            send_sem=q_send_sem.at[h * side + step],
-            recv_sem=q_recv_sem.at[h * side + src],
-            device_id=(q_ring[h](step), me_p),
-            device_id_type=MESH,
-        )
-
-    for step in (1, 3, 2):
-        for h in range(2):
-            q_copy(h, q_at[h], step).start()
-    for h in range(2):
-        v_copy(h, key_block(h, behind), 0, behind).wait_recv()
-        v_copy(h, key_block(h, behind), 2, ahead).start()
-
     w_half = tok // 2
 
     def w_copy(i, block, lo, size, peer):
@@ -325,32 +313,36 @@
     w_copy(1, me_p, 0, tok, left).start()
     w_copy(2, me_p, 0, tok, sib).start()
 
+    project(far)
+    row_copy(7, sib_far, None, sib).wait_recv()
+    project(sib_far)
+
+    query = jnp.dot(gather[...], q_pad[...], preferred_element_type=F32).astype(BF16)
+    q_buf[0, z] = query[:, 0:HD]
+    q_buf[1, y] = query[:, HD:]
+    q_ring = (along_z, along_y)
+    q_at = (z, y)
+
+    def q_copy(h, src, step):
+        return pltpu.make_async_remote_copy(
+            src_ref=q_buf.at[h, src],
+            dst_ref=q_buf.at[h, src],
+            send_sem=q_send_sem.at[h * side + step],
+            recv_sem=q_recv_sem.at[h * side + src],
+            device_id=(q_ring[h](step), me_p),
+            device_id_type=MESH,
+        )
+
+    for step in (1, 3, 2):
+        for h in range(2):
+            q_copy(h, q_at[h], step).start()
+    for h in range(2):
+        v_copy(h, key_block(h, behind), 0, behind).wait_recv()
+        v_copy(h, key_block(h, behind), 2, ahead).start()
+
     chunk = 512
+    tile = 256
     scale = LOG2E / math.sqrt(HD)
-    key_iota = lax.broadcasted_iota(jnp.int32, (chunk, routed), 0).astype(F32)
-
-    def attend(h, t, j, masked):
-        query = q_buf[h, t]
-        scores = []
-        for i in range(span // chunk):
-            s = jnp.dot(
-                kbuf[h, j, i * chunk : (i + 1) * chunk, :], query, preferred_element_type=F32
-            )
-            if masked:
-                s = jnp.where(key_iota <= rf - float(i * chunk), s, NEG)
-            scores.append(s)
-        peak = functools.reduce(
-            jnp.maximum, [jnp.max(s, axis=0, keepdims=True) for s in scores]
-        )
-        peak = peak * scale
-        out = 0.0
-        for i, s in enumerate(scores):
-            weights = jnp.exp2(s * scale - peak).astype(BF16)
-            out = out + jnp.dot(
-                vbuf[h, j, :, i * chunk : (i + 1) * chunk], weights, preferred_element_type=F32
-            )
-        total = out[HD : HD + 1]
-        return out[:HD] / total, peak + jnp.log2(total)
 
     def less(a, b):
         return (b - a + side - 1) // side
@@ -361,50 +353,128 @@
     def blend(h, one, two):
         return one + h * (two - one)
 
-    def visit(h, t, peak, den):
-        count = blend(h, y + less(z, t), side * less(y, t) + z * same(y, t))
-        span_q = blend(h, y * side + t, t * side + z)
-        wanted = pattern[pl.ds(span_q, 1), :]
-
-        def one(j, state):
-            peak, den = state
+    def step_in(h, t, j, own):
+        if own:
+            lane_k = lax.broadcasted_iota(jnp.int32, (tile, chunk), 1).astype(F32)
+        else:
+            span_q = blend(h, y * side + t, t * side + z)
             span_k = blend(h, j * side + z, y * side + j)
+            wanted = pattern[pl.ds(span_q, 1), :]
             hit = jnp.max(jnp.where(wanted == span_k, 1.0, 0.0), axis=1, keepdims=True)
-            out, lse = attend(h, t, j, False)
-            lse = jnp.where(hit > 0.5, lse, NEG)
-            top = jnp.maximum(peak, lse)
-            a = jnp.exp2(peak - top)
-            b = jnp.exp2(lse - top) * hit
-            acc[...] = acc[...] * a + out * b
-            return top, den * a + b
-
-        return lax.fori_loop(0, count, one, (peak, den))
+
+        def score(r, i):
+            s = lax.dot_general(
+                q_buf[h, t, r : r + tile, :],
+                kbuf[h, j, i : i + chunk, :],
+                (((1,), (1,)), ((), ())),
+                preferred_element_type=F32,
+            )
+            if own:
+                s = jnp.where(lane_k <= pos_col[r : r + tile, 0:1] - float(i), s, NEG)
+            return s
+
+        scores = [score(0, i) for i in range(0, span, chunk)]
+        for r in range(0, routed, tile):
+            peak = functools.reduce(
+                jnp.maximum, [jnp.max(s, axis=1, keepdims=True) for s in scores]
+            )
+            peak = peak * scale
+            later = []
+            out = 0.0
+            for n, i in enumerate(range(0, span, chunk)):
+                if r + tile < routed:
+                    later.append(score(r + tile, i))
+                weights = jnp.exp2(scores[n] * scale - peak).astype(BF16)
+                out = out + jnp.dot(
+                    weights, vbuf[h, j, i : i + chunk, :], preferred_element_type=F32
+                )
+            rows = slice(r, r + tile)
+            if own:
+                acc[h, t, rows, :] = out[:, 0:HD]
+                state[0, h, t, rows, :] = jnp.broadcast_to(peak, (tile, HD))
+                state[1, h, t, rows, :] = out[:, HD:]
+            else:
+                peak = jnp.where(hit > 0.5, peak, NEG)
+                former = state[0, h, t, rows, :]
+                top = jnp.maximum(former, peak)
+                a = jnp.exp2(former - top)
+                b = jnp.exp2(peak - top) * hit
+                acc[h, t, rows, :] = acc[h, t, rows, :] * a + out[:, 0:HD] * b
+                state[0, h, t, rows, :] = top
+                state[1, h, t, rows, :] = state[1, h, t, rows, :] * a + out[:, HD:] * b
+            scores = later
+
+    def slot(h, step):
+        return lax.rem(blend(h, z, y) + step, side)
+
+    def block(h, step):
+        return lax.rem(blend(h, y, z) + step, side)
+
+    def sees(h, t, j):
+        by_row = less(j, y) + same(j, y) * less(z, t)
+        by_col = less(y, t) + same(y, t) * less(j, z)
+        return blend(h, by_row, by_col)
 
     def begin(h, _):
-        out, lse = attend(h, blend(h, z, y), blend(h, y, z), True)
-        own[h] = out
-        own_st[h, 0:1, :] = lse
+        for step in range(1, side):
+            t = slot(h, step)
+            acc[h, t] = jnp.zeros((routed, HD), F32)
+            state[0, h, t] = jnp.full((routed, HD), NEG, F32)
+            state[1, h, t] = jnp.zeros((routed, HD), F32)
+        step_in(h, slot(h, 0), block(h, 0), True)
         return 0
 
     lax.fori_loop(0, 2, begin, 0)
+
+    def own_block(i, _):
+        step = 1 + i // 2
+        h = lax.rem(i, 2)
+        t = slot(h, step)
+        pltpu.make_async_remote_copy(
+            src_ref=q_buf.at[h, t],
+            dst_ref=q_buf.at[h, t],
+            send_sem=q_send_sem.at[h * side + step],
+            recv_sem=q_recv_sem.at[h * side + t],
+            device_id=(blend(h, along_z(step), along_y(step)), me_p),
+            device_id_type=MESH,
+        ).wait_recv()
+        j = block(h, 0)
+
+        @pl.when(sees(h, t, j) == 1)
+        def _():
+            step_in(h, t, j, False)
+
+        return 0
+
+    lax.fori_loop(0, 2 * (side - 1), own_block, 0)
 
     for h in range(2):
         k_copy(h, key_block(h, ahead), 0, ahead).wait_recv()
         v_copy(h, key_block(h, ahead), 0, ahead).wait_recv()
+
+    def near_blocks(i, _):
+        h = lax.rem(i, 2)
+        t = slot(h, lax.rem(i // 2, side))
+        j = block(h, 1 + 2 * (i // (2 * side)))
+
+        @pl.when(sees(h, t, j) == 1)
+        def _():
+            step_in(h, t, j, False)
+
+        return 0
+
+    lax.fori_loop(0, 4 * side, near_blocks, 0)
+
+    w_copy(0, left, 0, tok, right).wait_recv()
+    w_copy(3, left, 0, w_half, right).start()
+    w_copy(4, left, 0, tok, sib).start()
+    w_copy(1, right, 0, tok, left).wait_recv()
+    w_copy(5, right, w_half, w_half, left).start()
+    w_copy(6, right, 0, tok, sib).start()
+
+    for h in range(2):
         k_copy(h, key_block(h, 2), 0, behind).wait_recv()
         v_copy(h, key_block(h, 2), 0, behind).wait_recv()
-
-    ones = jnp.ones((1, routed), F32)
-
-    def finish_own(h, _):
-        acc[...] = own[h]
-        peak, den = visit(h, blend(h, z, y), own_st[h, 0:1, :], ones)
-        own[h] = acc[...]
-        own_st[h, 0:1, :] = peak
-        own_st[h, 1:2, :] = den
-        return 0
-
-    lax.fori_loop(0, 2, finish_own, 0)
 
     def o_copy(h, src, dst):
         return pltpu.make_async_remote_copy(
@@ -426,49 +496,48 @@
             device_id_type=MESH,
         )
 
-    def serve(i, _):
-        step = i // 2
+    def far_block(i, _):
         h = lax.rem(i, 2)
-        at = blend(h, z, y)
-        t = lax.rem(at + step, side)
-        pltpu.make_async_remote_copy(
-            src_ref=q_buf.at[h, t],
-            dst_ref=q_buf.at[h, t],
-            send_sem=q_send_sem.at[h * side + step],
-            recv_sem=q_recv_sem.at[h * side + t],
-            device_id=(blend(h, along_z(step), along_y(step)), me_p),
-            device_id_type=MESH,
-        ).wait_recv()
-        acc[...] = jnp.zeros((HD, routed), F32)
-        peak, den = visit(h, t, ones * NEG, ones * 0.0)
-        o_send[h, t] = (acc[...] / jnp.where(den > 0.0, den, 1.0)).astype(BF16)
-        st_send[h, t] = jnp.broadcast_to(
-            jnp.where(den > 0.0, peak + jnp.log2(den), NEG), (8, routed)
-        )
+        turn = i // 2
+        step = lax.rem(turn + 1, side - 1) + 1
+        at = slot(h, 0)
+        t = slot(h, step)
+        j = block(h, 2)
+
+        @pl.when(sees(h, t, j) == 1)
+        def _():
+            step_in(h, t, j, False)
+
+        den = state[1, h, t]
+        o_send[h, t] = (acc[h, t] / jnp.where(den > 0.0, den, 1.0)).astype(BF16)
+        lse = jnp.where(den > 0.0, state[0, h, t] + jnp.log2(den), NEG)
+        st_send[h, t] = jnp.transpose(lse)[0:8]
         o_copy(h, at, t).start()
         s_copy(h, at, t).start()
         return 0
 
-    lax.fori_loop(2, 6, serve, 0)
-
-    w_copy(0, left, 0, tok, right).wait_recv()
-    w_copy(3, left, 0, w_half, right).start()
-    w_copy(4, left, 0, tok, sib).start()
-    w_copy(1, right, 0, tok, left).wait_recv()
-    w_copy(5, right, w_half, w_half, left).start()
-    w_copy(6, right, 0, tok, sib).start()
-
-    lax.fori_loop(6, 2 * side, serve, 0)
+    lax.fori_loop(0, 2 * (side - 1), far_block, 0)
+
+    def far_own(h, _):
+        t = slot(h, 0)
+        j = block(h, 2)
+
+        @pl.when(sees(h, t, j) == 1)
+        def _():
+            step_in(h, t, j, False)
+
+        return 0
+
+    lax.fori_loop(0, 2, far_own, 0)
 
     w_copy(3, far, 0, w_half, right).wait_recv()
     w_copy(5, far, w_half, w_half, left).wait_recv()
     w_copy(7, far, 0, tok, sib).start()
 
     slot_rows = pl.ds(pl.multiple_of(me_p * per_slot, per_slot), per_slot)
-    from_pad = lax.dot_general(
-        slot_of[slot_rows, :], spread[...], (((1,), (1,)), ((), ())), preferred_element_type=F32
+    from_pad = jnp.dot(
+        slot_of[slot_rows, :], gather[...], preferred_element_type=F32
     ).astype(BF16)
-    flat = n_pack * cap
     for n in range(0, width, 512):
         picked = 0.0
         for b in range(n_pack):
@@ -484,26 +553,22 @@
     )
 
     for h in range(2):
-        peak, den = own_st[h, 0:1, :], own_st[h, 1:2, :]
-        total = own[h]
-        for step in (3, 2, 1):
+        peak, den = state[0, h, q_at[h]], state[1, h, q_at[h]]
+        total = acc[h, q_at[h]]
+        for step in (2, 1, 3):
             src = lax.rem(q_at[h] + step, side)
             o_copy(h, src, q_at[h]).wait_recv()
             s_copy(h, src, q_at[h]).wait_recv()
-            lse = st_in[h, src, 0:1, :]
+            lse = jnp.transpose(jnp.broadcast_to(st_in[h, src, 0:1, :], (HD, routed)))
             top = jnp.maximum(peak, lse)
             a = jnp.exp2(peak - top)
             b = jnp.exp2(lse - top)
             total = total * a + o_in[h, src].astype(F32) * b
             peak, den = top, den * a + b
-        att[h * HD : (h + 1) * HD, :] = (total / den).astype(BF16)
-
-    by_slot = lax.dot_general(
-        slot_of[...], att[...], (((1,), (1,)), ((), ())), preferred_element_type=F32
-    ).astype(BF16)
-    by_owner = lax.dot_general(
-        spread[...], att[...], (((1,), (1,)), ((), ())), preferred_element_type=F32
-    ).astype(BF16)
+        att[:, h * HD : (h + 1) * HD] = (total / den).astype(BF16)
+
+    by_slot = jnp.dot(slot_of[...], att[...], preferred_element_type=F32).astype(BF16)
+    by_owner = jnp.dot(spread[...], att[...], preferred_element_type=F32).astype(BF16)
     for d in range(n_pack):
         a_send[d, 0:per_slot, :] = by_slot[d * per_slot : (d + 1) * per_slot]
         a_send[d, per_slot:, :] = by_owner[d * cap : (d + 1) * cap]
@@ -614,18 +679,19 @@
             pltpu.VMEM((n_pack, cap, width), BF16),
             pltpu.VMEM((n_pack * cap, heads), BF16),
             pltpu.VMEM((n_pack * cap, routed), BF16),
+            pltpu.VMEM((routed, n_pack * cap), BF16),
             pltpu.VMEM((routed, routed), BF16),
+            pltpu.VMEM((routed, HD), F32),
             pltpu.VMEM((2, side, span, HD), BF16),
-            pltpu.VMEM((2, side, HD + 16, span), BF16),
-            pltpu.VMEM((2, side, HD, routed), BF16),
-            pltpu.VMEM((2, side, HD, routed), BF16),
-            pltpu.VMEM((2, side, HD, routed), BF16),
+            pltpu.VMEM((2, side, span, 2 * HD), BF16),
+            pltpu.VMEM((2, side, routed, HD), BF16),
+            pltpu.VMEM((2, side, routed, HD), BF16),
+            pltpu.VMEM((2, side, routed, HD), BF16),
             pltpu.VMEM((2, side, 8, routed), F32),
             pltpu.VMEM((2, side, 8, routed), F32),
-            pltpu.VMEM((2, HD, routed), F32),
-            pltpu.VMEM((2, 8, routed), F32),
-            pltpu.VMEM((HD, routed), F32),
-            pltpu.VMEM((heads, routed), BF16),
+            pltpu.VMEM((2, side, routed, HD), F32),
+            pltpu.VMEM((2, 2, side, routed, HD), F32),
+            pltpu.VMEM((routed, heads), BF16),
             pltpu.VMEM((n_pack * tok, width), BF16),
             pltpu.VMEM((n_pack, both, heads), BF16),
             pltpu.VMEM((n_pack, both, heads), BF16),

time: 109 us -> 97.3 us (0.89)
  the two profiles are of different devices: /device:TPU:41 before, /device:TPU:1 now
where the time goes in v3:
time: 97.3 us; the launch traced here: 96 us
  Pallas kernels  92.3 us (95%)
  local copies, waits for them, and re-layouts  3.05 us (3%)
    pallas_call x1, Pallas kernels, local(): pl.pallas_call(functools.partial(body, n_ctx, n_pack), out_shape=(jax.Sha...  92.3 us
    unnamed x4, local copies, waits for them, and re-layouts  3.05 us

profile of v3, /device:TPU:1, one launch (start us, length us, event | category | flops | bytes accessed | tf_op | source)
XLA Modules:
  0.0 96.0 jit_solution(9968995122230421119)
XLA Ops:
  0.6 92.3 %routed_attention.1 = (bf16[256,2048]{1,0:T(8,128)(2,1)}, bf16[64,2048]{1,0:T(8,128)(2,1)}) custom-call(bf16[256,2048]{1,0:T(8,128)(2,1)} %hidden.1, bf16[2048,256]{1,0:T(8,128)(2,1)} %keys.1, bf16[2048,256]{1,0:T(8,128)(2,1)} %values.1, bf16[2048,256]{1,0:T(8,128)(2,1)} %w_query.1, bf16[256,2048]{1,0:T(8,128)(2,1)} %w_out.1, f32[1,2048]{1,0:T(1,128)} %bitcast.2, ...), custom_call_target="tpu_custom_call" | custom-call | tf_op jit(solution)/shard_map/routed_attention/pallas_call | solution.py:670
  92.9 0.0 copy-start
  92.9 2.3 %copy.15 = bf16[256,2048]{1,0:T(8,128)(2,1)} copy(bf16[256,2048]{1,0:T(8,128)(2,1)} %get-tuple-element.4) | data formatting | bytes 2097152
  95.3 0.0 copy-done
  95.3 0.7 copy.16
Async XLA Ops:
  92.9 2.4 %copy-start = (bf16[64,2048]{1,0:T(8,128)(2,1)S(1)}, bf16[64,2048]{1,0:T(8,128)(2,1)}, u32[]{:S(2)}) copy-start(bf16[64,2048]{1,0:T(8,128)(2,1)} %get-tuple-element.5) | copy-start | bytes 786436

commit v4 on v3

--- a/solution.py
+++ b/solution.py
@@ -82,6 +82,8 @@
     w_all,
     a_send,
     a_in,
+    relay,
+    mix,
     res,
     gate,
     row_send,
@@ -98,6 +100,8 @@
     s_recv_sem,
     a_send_sem,
     a_recv_sem,
+    r_send_sem,
+    r_recv_sem,
     loc_sem,
 ):
     me_c = lax.axis_index("ctx")
@@ -282,9 +286,6 @@
     fwd_sib_right.start()
     project(left)
     project(right)
-    for h in range(2):
-        k_copy(h, key_block(h, behind), 0, behind).wait_recv()
-        k_copy(h, key_block(h, behind), 2, ahead).start()
     row_copy(2, sib, None, sib).wait_recv()
     project(sib)
     row_copy(4, sib_left, None, sib).wait_recv()
@@ -311,7 +312,6 @@
     own_w.wait()
     w_copy(0, me_p, 0, tok, right).start()
     w_copy(1, me_p, 0, tok, left).start()
-    w_copy(2, me_p, 0, tok, sib).start()
 
     project(far)
     row_copy(7, sib_far, None, sib).wait_recv()
@@ -333,12 +333,21 @@
             device_id_type=MESH,
         )
 
-    for step in (1, 3, 2):
+    for step in (1, 3):
         for h in range(2):
             q_copy(h, q_at[h], step).start()
-    for h in range(2):
-        v_copy(h, key_block(h, behind), 0, behind).wait_recv()
-        v_copy(h, key_block(h, behind), 2, ahead).start()
+    w_copy(2, me_p, 0, tok, sib).start()
+
+    def q_forward(h):
+        src = lax.rem(q_at[h] + behind, side)
+        return pltpu.make_async_remote_copy(
+            src_ref=q_buf.at[h, src],
+            dst_ref=q_buf.at[h, src],
+            send_sem=q_send_sem.at[h * side + 2],
+            recv_sem=q_recv_sem.at[h * side + src],
+            device_id=(q_ring[h](ahead), me_p),
+            device_id_type=MESH,
+        )
 
     chunk = 512
     tile = 256
@@ -426,18 +435,16 @@
 
     lax.fori_loop(0, 2, begin, 0)
 
+    for h in range(2):
+        q_copy(h, lax.rem(q_at[h] + behind, side), behind).wait_recv()
+        q_forward(h).start()
+    for h in range(2):
+        q_copy(h, lax.rem(q_at[h] + ahead, side), ahead).wait_recv()
+
     def own_block(i, _):
-        step = 1 + i // 2
         h = lax.rem(i, 2)
-        t = slot(h, step)
-        pltpu.make_async_remote_copy(
-            src_ref=q_buf.at[h, t],
-            dst_ref=q_buf.at[h, t],
-            send_sem=q_send_sem.at[h * side + step],
-            recv_sem=q_recv_sem.at[h * side + t],
-            device_id=(blend(h, along_z(step), along_y(step)), me_p),
-            device_id_type=MESH,
-        ).wait_recv()
+        turn = i // 2
+        t = slot(h, turn + turn // 2 - 2 * (turn // 3))
         j = block(h, 0)
 
         @pl.when(sees(h, t, j) == 1)
@@ -446,7 +453,17 @@
 
         return 0
 
-    lax.fori_loop(0, 2 * (side - 1), own_block, 0)
+    lax.fori_loop(2, 6, own_block, 0)
+
+    for h in range(2):
+        k_copy(h, key_block(h, behind), 0, behind).wait_recv()
+        k_copy(h, key_block(h, behind), 2, ahead).start()
+        v_copy(h, key_block(h, behind), 0, behind).wait_recv()
+        v_copy(h, key_block(h, behind), 2, ahead).start()
+    for h in range(2):
+        q_copy(h, lax.rem(q_at[h] + 2, side), behind).wait_recv()
+
+    lax.fori_loop(6, 8, own_block, 0)
 
     for h in range(2):
         k_copy(h, key_block(h, ahead), 0, ahead).wait_recv()
@@ -454,7 +471,8 @@
 
     def near_blocks(i, _):
         h = lax.rem(i, 2)
-        t = slot(h, lax.rem(i // 2, side))
+        turn = lax.rem(i // 2, side)
+        t = slot(h, turn + turn // 2 - 2 * (turn // 3))
         j = block(h, 1 + 2 * (i // (2 * side)))
 
         @pl.when(sees(h, t, j) == 1)
@@ -583,36 +601,75 @@
             device_id_type=MESH,
         )
 
-    def send_a(i, _):
-        a_copy(me_p, lax.rem(me_p + i, n_pack)).start()
-        return 0
-
-    lax.fori_loop(1, n_pack, send_a, 0)
-    a_in[me_p] = a_send[me_p]
-
+    def relay_copy(i, dst):
+        return pltpu.make_async_remote_copy(
+            src_ref=a_send.at[dst],
+            dst_ref=relay.at[i],
+            send_sem=r_send_sem.at[i],
+            recv_sem=r_recv_sem.at[i],
+            device_id=(me_c, left),
+            device_id_type=MESH,
+        )
+
+    def relay_on(i, dst):
+        return pltpu.make_async_remote_copy(
+            src_ref=relay.at[i],
+            dst_ref=a_in.at[right],
+            send_sem=r_send_sem.at[2 + i],
+            recv_sem=a_recv_sem.at[right],
+            device_id=(me_c, dst),
+            device_id_type=MESH,
+        )
+
+    @pl.when(core == 0)
+    def _():
+        a_copy(me_p, far).start()
+        a_copy(me_p, sib_far).start()
+
+    @pl.when(core == 1)
+    def _():
+        relay_copy(0, far).start()
+        relay_copy(1, sib_far).start()
+
+    a_copy(me_p, right).start()
+    a_copy(me_p, left).start()
+    a_copy(me_p, sib_right).start()
+    a_copy(me_p, sib_left).start()
+    a_copy(me_p, sib).start()
+
+    def add(rows, b, first):
+        for n in range(0, width, 512):
+            cols = slice(n, n + 512)
+            part = jnp.dot(
+                rows, w_all[pl.ds(b * tok, tok), cols], preferred_element_type=F32
+            )
+            mix[:, cols] = part if first else mix[:, cols] + part
+
+    add(a_send[me_p], me_p, True)
     w_copy(2, sib, 0, tok, sib).wait_recv()
+    a_copy(sib, me_p).wait_recv()
+    add(a_in[sib], sib, False)
+
+    @pl.when(core == 1)
+    def _():
+        relay_copy(0, far).wait_recv()
+        relay_on(0, left).start()
+        relay_copy(1, sib_far).wait_recv()
+        relay_on(1, sib_left).start()
+
     w_copy(4, sib_left, 0, tok, sib).wait_recv()
     w_copy(6, sib_right, 0, tok, sib).wait_recv()
     w_copy(7, sib_far, 0, tok, sib).wait_recv()
-
-    def take_a(i, _):
-        peer = lax.rem(me_p + i, n_pack)
-        a_copy(peer, me_p).wait_recv()
-        return 0
-
-    lax.fori_loop(1, n_pack, take_a, 0)
+    for b in (right, left, sib_right, sib_left, far, sib_far):
+        a_copy(b, me_p).wait_recv()
+        add(a_in[b], b, False)
 
     present = lax.dot_general(
         pick, jnp.ones((cap, HD), BF16), (((0,), (0,)), ((), ())), preferred_element_type=F32
     )[:, 0:1]
     for n in range(0, width, 512):
         cols = slice(n, n + 512)
-        mixed = 0.0
-        for b in range(n_pack):
-            mixed = mixed + jnp.dot(
-                a_in[b], w_all[b * tok : (b + 1) * tok, cols], preferred_element_type=F32
-            )
-        updated = (res[:, cols] + gate[:, 0:1] * mixed).astype(BF16)
+        updated = (res[:, cols] + gate[:, 0:1] * mix[:, cols]).astype(BF16)
         packed[:, cols] = updated[0:per_slot]
         placed = lax.dot_general(
             pick, updated[per_slot:], (((0,), (0,)), ((), ())), preferred_element_type=F32
@@ -643,17 +700,31 @@
         v_copy(h, key_at[h], 0, 1).wait_send()
         v_copy(h, key_at[h], 1, side - 1).wait_send()
         v_copy(h, key_block(h, behind), 2, ahead).wait_send()
+        q_copy(h, q_at[h], 1).wait_send()
+        q_copy(h, q_at[h], 3).wait_send()
+        q_forward(h).wait_send()
         for step in (1, 2, 3):
             dst = lax.rem(q_at[h] + step, side)
-            q_copy(h, q_at[h], step).wait_send()
             o_copy(h, q_at[h], dst).wait_send()
             s_copy(h, q_at[h], dst).wait_send()
 
-    def sent_a(i, _):
-        a_copy(me_p, lax.rem(me_p + i, n_pack)).wait_send()
-        return 0
-
-    lax.fori_loop(1, n_pack, sent_a, 0)
+    a_copy(me_p, right).wait_send()
+    a_copy(me_p, left).wait_send()
+    a_copy(me_p, sib_right).wait_send()
+    a_copy(me_p, sib_left).wait_send()
+    a_copy(me_p, sib).wait_send()
+
+    @pl.when(core == 0)
+    def _():
+        a_copy(me_p, far).wait_send()
+        a_copy(me_p, sib_far).wait_send()
+
+    @pl.when(core == 1)
+    def _():
+        relay_copy(0, far).wait_send()
+        relay_copy(1, sib_far).wait_send()
+        relay_on(0, left).wait_send()
+        relay_on(1, sib_left).wait_send()
 
 
 def local(n_ctx, n_pack, *args):
@@ -695,6 +766,8 @@
             pltpu.VMEM((n_pack * tok, width), BF16),
             pltpu.VMEM((n_pack, both, heads), BF16),
             pltpu.VMEM((n_pack, both, heads), BF16),
+            pltpu.VMEM((2, both, heads), BF16),
+            pltpu.VMEM((both, width), F32),
             pltpu.VMEM((both, width), F32),
             pltpu.VMEM((both, HD), F32),
             dma((8,)),
@@ -711,6 +784,8 @@
             dma((2 * side,)),
             dma((n_pack,)),
             dma((n_pack,)),
+            dma((4,)),
+            dma((2,)),
             dma,
         ],
         compiler_params=pltpu.CompilerParams(

time: 97.3 us -> 90 us (0.925)
  Pallas kernels: 92.3 us -> 84.9 us
    pallas_call x1, Pallas kernels: 92.3 us -> 84.9 us  [local(): pl.pallas_call(functools.partial(body, n_ctx, n_pack), out_shape=(jax.Sha...]
where the time goes in v4:
time: 90 us; the launch traced here: 88.6 us
  Pallas kernels  84.9 us (94%)
  local copies, waits for them, and re-layouts  3.05 us (3%)
    pallas_call x1, Pallas kernels, local(): pl.pallas_call(functools.partial(body, n_ctx, n_pack), out_shape=(jax.Sha...  84.9 us
    unnamed x4, local copies, waits for them, and re-layouts  3.05 us

profile of v4, /device:TPU:1, one launch (start us, length us, event | category | flops | bytes accessed | tf_op | source)
XLA Modules:
  0.0 88.6 jit_solution(3069915296758826649)
XLA Ops:
  0.6 84.9 %routed_attention.1 = (bf16[256,2048]{1,0:T(8,128)(2,1)}, bf16[64,2048]{1,0:T(8,128)(2,1)}) custom-call(bf16[256,2048]{1,0:T(8,128)(2,1)} %hidden.1, bf16[2048,256]{1,0:T(8,128)(2,1)} %keys.1, bf16[2048,256]{1,0:T(8,128)(2,1)} %values.1, bf16[2048,256]{1,0:T(8,128)(2,1)} %w_query.1, bf16[256,2048]{1,0:T(8,128)(2,1)} %w_out.1, f32[1,2048]{1,0:T(1,128)} %bitcast.2, ...), custom_call_target="tpu_custom_call" | custom-call | tf_op jit(solution)/shard_map/routed_attention/pallas_call | solution.py:741
  85.6 0.0 copy-start
  85.6 2.3 %copy.15 = bf16[256,2048]{1,0:T(8,128)(2,1)} copy(bf16[256,2048]{1,0:T(8,128)(2,1)} %get-tuple-element.4) | data formatting | bytes 2097152
  87.9 0.0 copy-done
  87.9 0.7 copy.16
Async XLA Ops:
  85.6 2.4 %copy-start = (bf16[64,2048]{1,0:T(8,128)(2,1)S(1)}, bf16[64,2048]{1,0:T(8,128)(2,1)}, u32[]{:S(2)}) copy-start(bf16[64,2048]{1,0:T(8,128)(2,1)} %get-tuple-element.5) | copy-start | bytes 786436

commit v5 on v4

--- a/solution.py
+++ b/solution.py
@@ -64,6 +64,7 @@
     hidden_out,
     packed,
     rows_all,
+    w_q,
     q_pad,
     spread,
     gather,
@@ -103,6 +104,7 @@
     r_send_sem,
     r_recv_sem,
     loc_sem,
+    kv_sem,
 ):
     me_c = lax.axis_index("ctx")
     me_p = lax.axis_index("pack")
@@ -149,6 +151,22 @@
     lax.fori_loop(1, n_pack, greet_pack, 0)
     lax.fori_loop(1, side, greet_ctx, 0)
 
+    own_w = pltpu.make_async_copy(w_out, w_all.at[pl.ds(me_p * tok, tok)], loc_sem)
+    own_q = pltpu.make_async_copy(w_query, w_q, kv_sem.at[4])
+    own_k = []
+    own_v = []
+    for h in range(2):
+        cols = pl.ds(h * HD, HD)
+        at = (y, z)[h]
+        own_k.append(pltpu.make_async_copy(keys.at[:, cols], kbuf.at[h, at], kv_sem.at[h]))
+        own_v.append(
+            pltpu.make_async_copy(
+                values.at[:, cols], vbuf.at[h, at, :, pl.ds(0, HD)], kv_sem.at[2 + h]
+            )
+        )
+    for copy in own_k + own_v + [own_q, own_w]:
+        copy.start()
+
     rf = routes[...].astype(F32)
     lane_i = lax.broadcasted_iota(jnp.int32, (cap, routed), 1).astype(F32)
     sub_j = lax.broadcasted_iota(jnp.int32, (cap, routed), 0).astype(F32)
@@ -216,11 +234,11 @@
         )
 
     for h in range(2):
-        kbuf[h, key_at[h]] = keys[:, h * HD : (h + 1) * HD]
+        own_k[h].wait()
         k_copy(h, key_at[h], 0, 1).start()
         k_copy(h, key_at[h], 1, side - 1).start()
     for h in range(2):
-        vbuf[h, key_at[h], :, 0:HD] = values[:, h * HD : (h + 1) * HD]
+        own_v[h].wait()
         v_copy(h, key_at[h], 0, 1).start()
         v_copy(h, key_at[h], 1, side - 1).start()
     for h in range(2):
@@ -230,8 +248,6 @@
     def key_block(h, step):
         return lax.rem(key_at[h] + step, side)
 
-    own_w = pltpu.make_async_copy(w_out, w_all.at[pl.ds(me_p * tok, tok)], loc_sem)
-    own_w.start()
 
     gain_row = gain[...]
     trig = table[...]
@@ -263,7 +279,7 @@
         rows = rows_all[block].astype(F32)
         mean_square = jnp.mean(rows * rows, axis=1, keepdims=True)
         normed = (rows * lax.rsqrt(mean_square + EPS) * gain_row).astype(BF16)
-        proj = jnp.dot(normed, w_query[...], preferred_element_type=F32)
+        proj = jnp.dot(normed, w_q[...], preferred_element_type=F32)
         _, pos = spread_of(block)
         cosine, sine = cos_sin(pos + base, trig)
         sine = sine * trig[2:3]
@@ -273,6 +289,7 @@
             turned = part * cosine + pltpu.roll(part, HD // 2, 1) * sine
             q_pad[pl.ds(start, cap), h * HD : (h + 1) * HD] = turned.astype(BF16)
 
+    own_q.wait()
     project(me_p)
     row_copy(0, left, None, right).wait_recv()
     fwd_right = row_copy(3, left, first, right)
@@ -481,7 +498,7 @@
 
         return 0
 
-    lax.fori_loop(0, 4 * side, near_blocks, 0)
+    lax.fori_loop(0, 3 * side, near_blocks, 0)
 
     w_copy(0, left, 0, tok, right).wait_recv()
     w_copy(3, left, 0, w_half, right).start()
@@ -489,6 +506,8 @@
     w_copy(1, right, 0, tok, left).wait_recv()
     w_copy(5, right, w_half, w_half, left).start()
     w_copy(6, right, 0, tok, sib).start()
+
+    lax.fori_loop(3 * side, 4 * side, near_blocks, 0)
 
     for h in range(2):
         k_copy(h, key_block(h, 2), 0, behind).wait_recv()
@@ -548,9 +567,6 @@
 
     lax.fori_loop(0, 2, far_own, 0)
 
-    w_copy(3, far, 0, w_half, right).wait_recv()
-    w_copy(5, far, w_half, w_half, left).wait_recv()
-    w_copy(7, far, 0, tok, sib).start()
 
     slot_rows = pl.ds(pl.multiple_of(me_p * per_slot, per_slot), per_slot)
     from_pad = jnp.dot(
@@ -645,6 +661,10 @@
             )
             mix[:, cols] = part if first else mix[:, cols] + part
 
+    w_copy(3, far, 0, w_half, right).wait_recv()
+    w_copy(5, far, w_half, w_half, left).wait_recv()
+    w_copy(7, far, 0, tok, sib).start()
+
     add(a_send[me_p], me_p, True)
     w_copy(2, sib, 0, tok, sib).wait_recv()
     a_copy(sib, me_p).wait_recv()
@@ -657,10 +677,10 @@
         relay_copy(1, sib_far).wait_recv()
         relay_on(1, sib_left).start()
 
-    w_copy(4, sib_left, 0, tok, sib).wait_recv()
-    w_copy(6, sib_right, 0, tok, sib).wait_recv()
-    w_copy(7, sib_far, 0, tok, sib).wait_recv()
-    for b in (right, left, sib_right, sib_left, far, sib_far):
+    late = {2: (6, sib_right), 3: (4, sib_left), 5: (7, sib_far)}
+    for n, b in enumerate((right, left, sib_right, sib_left, far, sib_far)):
+        if n in late:
+            w_copy(late[n][0], late[n][1], 0, tok, sib).wait_recv()
         a_copy(b, me_p).wait_recv()
         add(a_in[b], b, False)
 
@@ -744,10 +764,11 @@
             jax.ShapeDtypeStruct((tok, width), BF16),
             jax.ShapeDtypeStruct((per_slot, width), BF16),
         ),
-        in_specs=[vmem] * 11,
+        in_specs=[vmem] + [pl.BlockSpec(memory_space=pl.ANY)] * 4 + [vmem] * 6,
         out_specs=(vmem, vmem),
         scratch_shapes=[
             pltpu.VMEM((n_pack, cap, width), BF16),
+            pltpu.VMEM((width, heads), BF16),
             pltpu.VMEM((n_pack * cap, heads), BF16),
             pltpu.VMEM((n_pack * cap, routed), BF16),
             pltpu.VMEM((routed, n_pack * cap), BF16),
@@ -787,6 +808,7 @@
             dma((4,)),
             dma((2,)),
             dma,
+            dma((5,)),
         ],
         compiler_params=pltpu.CompilerParams(
             collective_id=0, has_side_effects=True, vmem_limit_bytes=60 << 20

time: 90 us -> 84.4 us (0.938); the launches traced: 88.6 us -> 84.3 us
  Pallas kernels: 84.9 us -> 80.5 us
    pallas_call x1, Pallas kernels: 84.9 us -> 80.5 us  [local(): pl.pallas_call(functools.partial(body, n_ctx, n_pack), out_shape=(jax.Sha...]
where the time goes in v5:
time: 84.4 us; the launch traced here: 84.3 us
  Pallas kernels  80.5 us (95%)
  local copies, waits for them, and re-layouts  3.05 us (4%)
    pallas_call x1, Pallas kernels, local(): pl.pallas_call(functools.partial(body, n_ctx, n_pack), out_shape=(jax.Sha...  80.5 us
    unnamed x4, local copies, waits for them, and re-layouts  3.05 us

profile of v5, /device:TPU:1, one launch (start us, length us, event | category | flops | bytes accessed | tf_op | source)
XLA Modules:
  0.0 84.3 jit_solution(4687728243668118153)
XLA Ops:
  0.6 80.5 %routed_attention.1 = (bf16[256,2048]{1,0:T(8,128)(2,1)}, bf16[64,2048]{1,0:T(8,128)(2,1)}) custom-call(bf16[256,2048]{1,0:T(8,128)(2,1)} %hidden.1, bf16[2048,256]{1,0:T(8,128)(2,1)} %keys.1, bf16[2048,256]{1,0:T(8,128)(2,1)} %values.1, bf16[2048,256]{1,0:T(8,128)(2,1)} %w_query.1, bf16[256,2048]{1,0:T(8,128)(2,1)} %w_out.1, f32[1,2048]{1,0:T(1,128)} %bitcast.2, ...), custom_call_target="tpu_custom_call" | custom-call | tf_op jit(solution)/shard_map/routed_attention/pallas_call | solution.py:761
  81.2 0.0 copy-start
  81.2 2.3 %copy.15 = bf16[256,2048]{1,0:T(8,128)(2,1)} copy(bf16[256,2048]{1,0:T(8,128)(2,1)} %get-tuple-element.4) | data formatting | bytes 2097152
  83.5 0.0 copy-done
  83.5 0.7 copy.16
Async XLA Ops:
  81.2 2.4 %copy-start = (bf16[64,2048]{1,0:T(8,128)(2,1)S(1)}, bf16[64,2048]{1,0:T(8,128)(2,1)}, u32[]{:S(2)}) copy-start(bf16[64,2048]{1,0:T(8,128)(2,1)} %get-tuple-element.5) | copy-start | bytes 786436

commit v6 on v5

--- a/solution.py
+++ b/solution.py
@@ -61,8 +61,8 @@
     order,
     pattern,
     table,
-    hidden_out,
-    packed,
+    fresh,
+    picked_out,
     rows_all,
     w_q,
     q_pad,
@@ -275,6 +275,8 @@
     lane_s = lax.broadcasted_iota(jnp.int32, (routed, routed), 1).astype(F32)
     slot_of[...] = jnp.where(lane_s == order_col, 1.0, 0.0).astype(BF16)
 
+    scale = LOG2E / math.sqrt(HD)
+
     def project(block):
         rows = rows_all[block].astype(F32)
         mean_square = jnp.mean(rows * rows, axis=1, keepdims=True)
@@ -287,7 +289,7 @@
         for h in range(2):
             part = proj[:, h * HD : (h + 1) * HD]
             turned = part * cosine + pltpu.roll(part, HD // 2, 1) * sine
-            q_pad[pl.ds(start, cap), h * HD : (h + 1) * HD] = turned.astype(BF16)
+            q_pad[pl.ds(start, cap), h * HD : (h + 1) * HD] = (turned * scale).astype(BF16)
 
     own_q.wait()
     project(me_p)
@@ -368,8 +370,6 @@
 
     chunk = 512
     tile = 256
-    scale = LOG2E / math.sqrt(HD)
-
     def less(a, b):
         return (b - a + side - 1) // side
 
@@ -399,21 +399,32 @@
                 s = jnp.where(lane_k <= pos_col[r : r + tile, 0:1] - float(i), s, NEG)
             return s
 
-        scores = [score(0, i) for i in range(0, span, chunk)]
+        def starts(r):
+            if not own:
+                return list(range(0, span, chunk))
+            return [
+                i
+                for i in range(0, span, chunk)
+                if r + tile > routed - cap * pl.cdiv(span - i, tok)
+            ]
+
+        scores = [score(0, i) for i in starts(0)]
         for r in range(0, routed, tile):
             peak = functools.reduce(
                 jnp.maximum, [jnp.max(s, axis=1, keepdims=True) for s in scores]
             )
-            peak = peak * scale
             later = []
+            ahead_of = starts(r + tile) if r + tile < routed else []
             out = 0.0
-            for n, i in enumerate(range(0, span, chunk)):
-                if r + tile < routed:
-                    later.append(score(r + tile, i))
-                weights = jnp.exp2(scores[n] * scale - peak).astype(BF16)
+            for n, i in enumerate(starts(r)):
+                if n < len(ahead_of):
+                    later.append(score(r + tile, ahead_of[n]))
+                weights = jnp.exp2(scores[n] - peak).astype(BF16)
                 out = out + jnp.dot(
                     weights, vbuf[h, j, i : i + chunk, :], preferred_element_type=F32
                 )
+            for i in ahead_of[len(later) :]:
+                later.append(score(r + tile, i))
             rows = slice(r, r + tile)
             if own:
                 acc[h, t, rows, :] = out[:, 0:HD]
@@ -684,17 +695,11 @@
         a_copy(b, me_p).wait_recv()
         add(a_in[b], b, False)
 
-    present = lax.dot_general(
-        pick, jnp.ones((cap, HD), BF16), (((0,), (0,)), ((), ())), preferred_element_type=F32
-    )[:, 0:1]
+    picked_out[...] = pick
     for n in range(0, width, 512):
         cols = slice(n, n + 512)
         updated = (res[:, cols] + gate[:, 0:1] * mix[:, cols]).astype(BF16)
-        packed[:, cols] = updated[0:per_slot]
-        placed = lax.dot_general(
-            pick, updated[per_slot:], (((0,), (0,)), ((), ())), preferred_element_type=F32
-        )
-        hidden_out[:, cols] = jnp.where(present > 0.5, placed.astype(BF16), hidden[:, cols])
+        fresh[:, cols] = updated
 
     to_right.wait_send()
     to_left.wait_send()
@@ -747,6 +752,18 @@
         relay_on(1, sib_left).wait_send()
 
 
+def place(hidden, fresh, pick, hidden_out, packed):
+    per_slot = packed.shape[0]
+    across = (((0,), (0,)), ((), ()))
+    chosen = pick[...]
+    present = lax.dot_general(
+        chosen, jnp.ones((chosen.shape[0], HD), BF16), across, preferred_element_type=F32
+    )[:, 0:1]
+    placed = lax.dot_general(chosen, fresh[per_slot:, :], across, preferred_element_type=F32)
+    hidden_out[...] = jnp.where(present > 0.5, placed.astype(BF16), hidden[...])
+    packed[...] = fresh[0:per_slot, :]
+
+
 def local(n_ctx, n_pack, *args):
     hidden, keys, values, w_query, w_out, gain, router, routes, order, pattern = args
     tok, width = hidden.shape
@@ -758,11 +775,11 @@
     side = math.isqrt(n_ctx)
     vmem = pl.BlockSpec(memory_space=pltpu.VMEM)
     dma = pltpu.SemaphoreType.DMA
-    return pl.pallas_call(
+    fresh, pick = pl.pallas_call(
         functools.partial(body, n_ctx, n_pack),
         out_shape=(
-            jax.ShapeDtypeStruct((tok, width), BF16),
-            jax.ShapeDtypeStruct((per_slot, width), BF16),
+            jax.ShapeDtypeStruct((both, width), BF16),
+            jax.ShapeDtypeStruct((cap, tok), BF16),
         ),
         in_specs=[vmem] + [pl.BlockSpec(memory_space=pl.ANY)] * 4 + [vmem] * 6,
         out_specs=(vmem, vmem),
@@ -827,6 +844,25 @@
         pattern,
         jnp.asarray(turn_table()),
     )
+    step = 1024
+    return pl.pallas_call(
+        place,
+        grid=(width // step,),
+        out_shape=(
+            jax.ShapeDtypeStruct((tok, width), BF16),
+            jax.ShapeDtypeStruct((per_slot, width), BF16),
+        ),
+        in_specs=[
+            pl.BlockSpec((tok, step), lambda n: (0, n)),
+            pl.BlockSpec((both, step), lambda n: (0, n)),
+            pl.BlockSpec((cap, tok), lambda n: (0, 0)),
+        ],
+        out_specs=(
+            pl.BlockSpec((tok, step), lambda n: (0, n)),
+            pl.BlockSpec((per_slot, step), lambda n: (0, n)),
+        ),
+        name="place_rows",
+    )(hidden, fresh, pick)
 
 
 def solution(mesh):

time: 84.4 us -> 83.3 us (0.987)
  local copies, waits for them, and re-layouts: 3.05 us -> 0 us
  Pallas kernels: 80.5 us -> 82.5 us
    unnamed x4 -> x0, local copies, waits for them, and re-layouts: 3.05 us -> none
    pallas_call x0 -> x1, Pallas kernels: none -> 2.76 us  [local(): pl.pallas_call(place, grid=(width // step,), out_shape=(jax.ShapeDtypeStr...]
where the time goes in v6:
time: 83.3 us; the launch traced here: 83.2 us
  Pallas kernels  82.5 us (99%)
    pallas_call x1, Pallas kernels, local(): pl.pallas_call(functools.partial(body, n_ctx, n_pack), out_shape=(jax.Sha...  79.8 us
    pallas_call x1, Pallas kernels, local(): pl.pallas_call(place, grid=(width // step,), out_shape=(jax.ShapeDtypeStr...  2.76 us

profile of v6, /device:TPU:1, one launch (start us, length us, event | category | flops | bytes accessed | tf_op | source)
XLA Modules:
  0.0 83.2 jit_solution(5709634380561760311)
XLA Ops:
  0.6 79.8 %routed_attention.1 = (bf16[160,2048]{1,0:T(8,128)(2,1)}, bf16[96,256]{1,0:T(8,128)(2,1)}) custom-call(bf16[256,2048]{1,0:T(8,128)(2,1)} %hidden.3, bf16[2048,256]{1,0:T(8,128)(2,1)} %keys.1, bf16[2048,256]{1,0:T(8,128)(2,1)} %values.1, bf16[2048,256]{1,0:T(8,128)(2,1)} %w_query.1, bf16[256,2048]{1,0:T(8,128)(2,1)} %w_out.1, f32[1,2048]{1,0:T(1,128)} %bitcast.2, ...), custom_call_target="tpu_custom_call" | custom-call | tf_op jit(solution)/shard_map/routed_attention/pallas_call | solution.py:778
  80.4 2.8 %place_rows.1 = (bf16[256,2048]{1,0:T(8,128)(2,1)}, bf16[64,2048]{1,0:T(8,128)(2,1)}) custom-call(bf16[256,2048]{1,0:T(8,128)(2,1)} %hidden.3, bf16[160,2048]{1,0:T(8,128)(2,1)} %get-tuple-element.4.fresh, bf16[96,256]{1,0:T(8,128)(2,1)} %get-tuple-element.5.pick), custom_call_target="tpu_custom_call" | custom-call | tf_op jit(solution)/shard_map/place_rows/pallas_call | solution.py:848

commit v7 on v6

--- a/solution.py
+++ b/solution.py
@@ -844,7 +844,7 @@
         pattern,
         jnp.asarray(turn_table()),
     )
-    step = 1024
+    step = width
     return pl.pallas_call(
         place,
         grid=(width // step,),

time: 83.3 us -> 83.5 us (level)
  no operation moved by 1% of the time
where the time goes in v7:
time: 83.5 us; the launch traced here: 83.3 us
  Pallas kernels  82.7 us (99%)
    pallas_call x1, Pallas kernels, local(): pl.pallas_call(functools.partial(body, n_ctx, n_pack), out_shape=(jax.Sha...  79.8 us
    pallas_call x1, Pallas kernels, local(): pl.pallas_call(place, grid=(width // step,), out_shape=(jax.ShapeDtypeStr...  2.93 us

profile of v7, /device:TPU:1, one launch (start us, length us, event | category | flops | bytes accessed | tf_op | source)
XLA Modules:
  0.0 83.3 jit_solution(11336379878984229149)
XLA Ops:
  0.6 79.8 %routed_attention.1 = (bf16[160,2048]{1,0:T(8,128)(2,1)}, bf16[96,256]{1,0:T(8,128)(2,1)}) custom-call(bf16[256,2048]{1,0:T(8,128)(2,1)} %hidden.3, bf16[2048,256]{1,0:T(8,128)(2,1)} %keys.1, bf16[2048,256]{1,0:T(8,128)(2,1)} %values.1, bf16[2048,256]{1,0:T(8,128)(2,1)} %w_query.1, bf16[256,2048]{1,0:T(8,128)(2,1)} %w_out.1, f32[1,2048]{1,0:T(1,128)} %bitcast.2, ...), custom_call_target="tpu_custom_call" | custom-call | tf_op jit(solution)/shard_map/routed_attention/pallas_call | solution.py:778
  80.4 2.9 %place_rows.1 = (bf16[256,2048]{1,0:T(8,128)(2,1)}, bf16[64,2048]{1,0:T(8,128)(2,1)}) custom-call(bf16[256,2048]{1,0:T(8,128)(2,1)} %hidden.3, bf16[160,2048]{1,0:T(8,128)(2,1)} %get-tuple-element.4.fresh, bf16[96,256]{1,0:T(8,128)(2,1)} %get-tuple-element.5.pick), custom_call_target="tpu_custom_call" | custom-call | tf_op jit(solution)/shard_map/place_rows/pallas_call | solution.py:848
